TPU v7x, 32 devices: a whole 2x2x4 slice. The times are simulated.
32 devices in a mesh: ctx: 8 (over z, x), grp: 4 (over y, core).
Axes of the slice: x: 2, y: 2, z: 4, core: 2. Of those that a mesh axis runs over, the one named last changes fastest.
Arguments:
- queries: bfloat16 [1024, 12288], P('ctx', 'grp'), parts along dimension 1, may hold values from -250 to 250
- keys: bfloat16 [2, 1024, 768], P(None, 'ctx', 'grp'), parts along dimension 2, may hold values from -6 to 6
- values: bfloat16 [2, 1024, 512], P(None, 'ctx', 'grp'), parts along dimension 2, may hold values from -6 to 6
- gate_logits: bfloat16 [1024, 192], P('ctx', 'grp'), parts along dimension 1, may hold values from -6 to 6
- sel_ids: int32 [64, 64], P('ctx', 'grp'), parts along dimension 1, may hold values from -1 to 31, as said below
- pos_k: bfloat16 [32, 768], P(None, 'grp'), parts along dimension 1, may hold values from -1 to 1
- pos_v: bfloat16 [32, 512], P(None, 'grp'), parts along dimension 1, may hold values from -1 to 1
- mix_k: bfloat16 [192, 768], P(None, 'grp'), parts along dimension 1, may hold values from -0.4375 to 0.4375
- mix_v: bfloat16 [128, 512], P(None, 'grp'), parts along dimension 1, may hold values from -0.5 to 0.5
Outputs:
- attended: bfloat16 [1024, 8192], P('ctx', 'grp'), parts along dimension 1
There are 4 independent parts, one for each index of `grp`. A program takes and returns all parts, laid end to end along the dimension named above; each array names one. Nothing has to cross between parts.
Inputs may be any that keep to these rules, and one draw needn't show every extreme that they name: `sel_ids`: the first entry of a row is the block that holds the row's tokens. The other entries name distinct blocks that lie wholly before position 1024, or are -1 at the row's end; each row has at least 12 entries that are not -1. Over the 8 rows of one device, the entries after the first name at most 16 = min(64, 1 * 2 * 8) distinct blocks, at most 2 of them held by one device, and no block in more than 8 rows.
All inputs are finite; a program needn't handle non-finite values.
Results may differ from a plain program's by a relative error of at most 0.011.
Values may be sent and summed in bfloat16 or wider, within the bound.
No kernel may reach another device: no remote copies, remote signals or barrier semaphores. Data moves between devices by JAX's collectives and lax.ppermute only.
A program may use at most 128 MiB of HBM per device.

v0:
```python
import jax
import jax.numpy as jnp
from jax import lax
from jax.sharding import PartitionSpec as P

HEADS = 16
DK = 192
DV = 128
CMP_BLOCK = 32
SEL_BLOCK = 64
QBLOCK = 16
SPREAD = 64


def shifted(value, axis, steps):
    count = lax.axis_size(axis)
    pairs = [(source, (source + steps) % count) for source in range(count)]
    return lax.ppermute(value, axis, pairs)


def attention(query_rows, key_rows, value_rows, allowed, head_count):
    scores = jnp.dot(query_rows, key_rows.T, preferred_element_type=jnp.float32) * query_rows.shape[
        1
    ] ** (-0.5)
    scores = scores.reshape(-1, head_count, key_rows.shape[0])
    scores = jnp.where(allowed[:, None, :], scores, -jnp.inf)
    highest = jnp.max(scores, axis=2, keepdims=True)
    weights = jnp.exp(scores - highest)
    totals = jnp.sum(weights, axis=2)
    rounded = weights.astype(jnp.bfloat16).reshape(-1, key_rows.shape[0])
    mixture = jnp.dot(rounded, value_rows, preferred_element_type=jnp.float32)
    return mixture.reshape(-1, head_count, value_rows.shape[1]) / totals[:, :, None]


def body(queries, keys, values, gate_logits, sel_ids, pos_k, pos_v, mix_k, mix_v):
    devices = lax.axis_size("ctx")
    myself = lax.axis_index("ctx")
    rounds = keys.shape[0]
    cached = rounds - 1
    tokens = keys.shape[1]
    scaling = DK ** (-0.5)
    query_rows = queries.reshape(tokens * HEADS, DK)
    query_pos = (cached * devices + myself) * tokens + jnp.arange(tokens, dtype=jnp.int32)
    paired = jnp.concatenate([keys, values], axis=2)
    earlier_rows = []
    for shift_by in range(1, 5):
        wrapped = myself + shift_by >= devices
        outgoing = jnp.where(wrapped, paired[0], paired[1])
        earlier_rows.append(shifted(outgoing, "ctx", shift_by))
    per_piece = tokens // CMP_BLOCK
    local_count = rounds * per_piece
    pooled_k = jnp.einsum(
        "bjd,jd->bd",
        keys.reshape(local_count, CMP_BLOCK, DK),
        pos_k,
        preferred_element_type=jnp.float32,
    ).astype(jnp.bfloat16)
    pooled_v = jnp.einsum(
        "bjd,jd->bd",
        values.reshape(local_count, CMP_BLOCK, DV),
        pos_v,
        preferred_element_type=jnp.float32,
    ).astype(jnp.bfloat16)
    comp_keys = jnp.dot(pooled_k, mix_k, preferred_element_type=jnp.float32).astype(jnp.bfloat16)
    comp_values = jnp.dot(pooled_v, mix_v, preferred_element_type=jnp.float32).astype(jnp.bfloat16)
    all_keys, all_values = (
        lax.all_gather(comp_keys, "ctx", axis=0, tiled=True),
        lax.all_gather(comp_values, "ctx", axis=0, tiled=True),
    )
    length = all_keys.shape[0]
    summed = jnp.zeros((tokens, HEADS, DV), jnp.float32)
    highest = jnp.full((tokens, HEADS), -jnp.inf, jnp.float32)
    totals = jnp.zeros((tokens, HEADS), jnp.float32)
    for low_row in range(0, length, 512):
        high_row = min(length, low_row + 512)
        key_index = low_row + jnp.arange(high_row - low_row, dtype=jnp.int32)
        holder = key_index // local_count
        within = key_index % local_count
        end_pos = (
            (within // per_piece * devices + holder) * tokens
            + (within % per_piece + 1) * CMP_BLOCK
            - 1
        )
        allowed = end_pos[None, :] <= query_pos[:, None]
        scores = (
            jnp.dot(query_rows, all_keys[low_row:high_row].T, preferred_element_type=jnp.float32)
            * scaling
        )
        scores = jnp.where(
            allowed[:, None, :], scores.reshape(tokens, HEADS, high_row - low_row), -jnp.inf
        )
        raised = jnp.maximum(highest, jnp.max(scores, axis=2))
        anchor = jnp.where(raised == -jnp.inf, 0.0, raised)
        weights = jnp.exp(scores - anchor[:, :, None])
        factor = jnp.exp(highest - anchor)
        totals = totals * factor + jnp.sum(weights, axis=2)
        mixture = jnp.dot(
            weights.astype(jnp.bfloat16).reshape(tokens * HEADS, high_row - low_row),
            all_values[low_row:high_row],
            preferred_element_type=jnp.float32,
        )
        summed = summed * factor[:, :, None] + mixture.reshape(tokens, HEADS, DV)
        highest = raised
    compressed = summed / totals[:, :, None]
    window_rows = jnp.concatenate(earlier_rows[::-1] + [paired[1]], axis=0)
    column = jnp.arange(5 * tokens, dtype=jnp.int32)[None, :]
    offsets = jnp.arange(tokens, dtype=jnp.int32)[:, None]
    inside = (column > offsets) & (column <= 4 * tokens + offsets)
    sliding = attention(query_rows, window_rows[:, :DK], window_rows[:, DK:], inside, HEADS)
    per_block = tokens // SEL_BLOCK
    groups = sel_ids.shape[0]
    listed = sel_ids.shape[1]
    remote = sel_ids[:, 1:].reshape(-1)
    entries = remote.shape[0]
    usable = remote >= 0
    clipped = jnp.maximum(remote, 0)
    holder_piece = clipped // per_block
    holder = holder_piece % devices
    local_block = holder_piece // devices * per_block + clipped % per_block
    distinct = min(SPREAD, cached * per_block * devices)
    per_owner = -(-distinct // devices)
    earlier = jnp.arange(entries)[None, :] < jnp.arange(entries)[:, None]
    same_owner = holder[:, None] == holder[None, :]
    key_blocks = keys.reshape(rounds * per_block, SEL_BLOCK, DK)
    value_blocks = values.reshape(rounds * per_block, SEL_BLOCK, DV)
    repeated = (remote[:, None] == remote[None, :]) & usable[None, :] & earlier
    leading = usable & ~jnp.any(repeated, axis=1)
    before = same_owner & leading[None, :] & earlier
    slot_of = holder * per_owner + jnp.sum(before, axis=1)
    first_seen = jnp.argmax(repeated, axis=1)
    fetch_at = jnp.where(leading, slot_of, slot_of[first_seen])
    target = jnp.where(leading, slot_of, devices * per_owner)
    requests = (
        jnp.full((devices * per_owner,), -1, jnp.int32).at[target].set(local_block, mode="drop")
    )
    wanted = lax.all_to_all(
        requests.reshape(devices, per_owner), "ctx", split_axis=0, concat_axis=0, tiled=True
    )
    chosen = jnp.maximum(wanted, 0)
    out_keys = key_blocks[chosen].reshape(devices, per_owner, SEL_BLOCK * DK)
    out_values = value_blocks[chosen].reshape(devices, per_owner, SEL_BLOCK * DV)
    got_keys, got_values = (
        lax.all_to_all(out_keys, "ctx", split_axis=0, concat_axis=0, tiled=True),
        lax.all_to_all(out_values, "ctx", split_axis=0, concat_axis=0, tiled=True),
    )
    near_keys = got_keys.reshape(devices * per_owner, SEL_BLOCK, DK)[fetch_at]
    near_values = got_values.reshape(devices * per_owner, SEL_BLOCK, DV)[fetch_at]
    own_index = cached * per_block + jnp.arange(groups, dtype=jnp.int32) * QBLOCK // SEL_BLOCK
    block_keys = jnp.concatenate(
        [key_blocks[own_index][:, None], near_keys.reshape(groups, listed - 1, SEL_BLOCK, DK)],
        axis=1,
    )
    block_values = jnp.concatenate(
        [value_blocks[own_index][:, None], near_values.reshape(groups, listed - 1, SEL_BLOCK, DV)],
        axis=1,
    )
    key_count = listed * SEL_BLOCK
    block_keys = block_keys.reshape(groups, key_count, DK)
    block_values = block_values.reshape(groups, key_count, DV)
    own_pos = (own_index - cached * per_block)[:, None] * SEL_BLOCK + jnp.arange(
        SEL_BLOCK, dtype=jnp.int32
    )[None, :]
    query_off = (
        jnp.arange(groups, dtype=jnp.int32)[:, None] * QBLOCK
        + jnp.arange(QBLOCK, dtype=jnp.int32)[None, :]
    )
    own_allowed = own_pos[:, None, :] <= query_off[:, :, None]
    far_allowed = jnp.repeat(usable.reshape(groups, listed - 1), SEL_BLOCK, axis=1)
    allowed = jnp.concatenate(
        [
            own_allowed,
            jnp.broadcast_to(far_allowed[:, None, :], (groups, QBLOCK, (listed - 1) * SEL_BLOCK)),
        ],
        axis=2,
    )
    grouped_q = queries.reshape(groups, QBLOCK * HEADS, DK)
    scores = (
        jnp.einsum("aqd,akd->aqk", grouped_q, block_keys, preferred_element_type=jnp.float32)
        * scaling
    )
    scores = jnp.where(
        allowed[:, :, None, :], scores.reshape(groups, QBLOCK, HEADS, key_count), -jnp.inf
    )
    sel_highest = jnp.max(scores, axis=3, keepdims=True)
    weights = jnp.exp(scores - sel_highest)
    sel_totals = jnp.sum(weights, axis=3)
    mixture = jnp.einsum(
        "aqk,akd->aqd",
        weights.astype(jnp.bfloat16).reshape(groups, QBLOCK * HEADS, key_count),
        block_values,
        preferred_element_type=jnp.float32,
    )
    selected = mixture.reshape(tokens, HEADS, DV) / sel_totals.reshape(tokens, HEADS)[:, :, None]
    gate_values = jax.nn.sigmoid(gate_logits.astype(jnp.float32)).reshape(tokens, 3, HEADS)
    combined = (
        gate_values[:, 0, :, None] * compressed
        + gate_values[:, 1, :, None] * selected
        + gate_values[:, 2, :, None] * sliding
    )
    return combined.reshape(tokens, HEADS * DV).astype(jnp.bfloat16)


def solution(mesh):
    in_specs = (
        P("ctx", "grp"),
        P(None, "ctx", "grp"),
        P(None, "ctx", "grp"),
        P("ctx", "grp"),
        P("ctx", "grp"),
        P(None, "grp"),
        P(None, "grp"),
        P(None, "grp"),
        P(None, "grp"),
    )
    out_specs = P("ctx", "grp")
    return jax.shard_map(body, mesh=mesh, in_specs=in_specs, out_specs=out_specs, check_vma=False)
```

profile of v0, /device:TPU:0, one launch (start us, length us, event | category | flops | bytes accessed | tf_op | source)
XLA Modules:
  0.0 185.5 jit_solution(2495808764564656676)
XLA Ops:
  3.7 1.2 gather_fusion.2
  5.0 0.9 scatter_custom_fusion
  6.6 7.3 %all-to-all-start = ((s32[8,1,2]{2,1,0:T(1,128)}), s32[8,1,2]{2,1,0:T(1,128)}, u32[]{:S(2)}, u32[]{:S(2)}) async-start(s32[8,1,2]{2,1,0:T(1,128)} %bitcast.23), calls=%async_computation | async-start | bytes 8192 | tf_op jit(solution)/shard_map/all_to_all | solution.py:136
  13.9 1.0 copy.57
  14.9 1.5 broadcast_select_fusion
  17.2 2.9 %collective-permute-start = (bf16[128,320]{1,0:T(8,128)(2,1)}, bf16[128,320]{1,0:T(8,128)(2,1)}, u32[]{:S(2)}, u32[]{:S(2)}) collective-permute-start(bf16[128,320]{1,0:T(8,128)(2,1)} %get-tuple-element.20), channel_id=1, source_target_pairs={{0,16},{4,20},{8,24},{12,28},{16,0},{20,4},{24,8},{28,12},{1,17},{... | collective-permute-start | bytes 245768 | tf_op jit(solution)/shard_map/ppermute | solution.py:18
  20.1 2.4 %collective-permute-start.1 = (bf16[128,320]{1,0:T(8,128)(2,1)}, bf16[128,320]{1,0:T(8,128)(2,1)}, u32[]{:S(2)}, u32[]{:S(2)}) collective-permute-start(bf16[128,320]{1,0:T(8,128)(2,1)} %get-tuple-element.19), channel_id=1, source_target_pairs={{0,12},{4,16},{8,20},{12,24},{16,28},{20,0},{24,4},{28,8},{1,13},{... | collective-permute-start | bytes 245768 | tf_op jit(solution)/shard_map/ppermute | solution.py:18
  22.4 1.1 collective-permute-start.3
  23.6 3.0 %reshape.574 = bf16[8,256,192]{2,1,0:T(8,128)(2,1)} reshape(bf16[128,3072]{1,0:T(8,128)(2,1)} %param.9) | data formatting | bytes 1572864 | tf_op jit(solution)/shard_map/reshape | solution.py:176
  26.6 1.1 reshape.567
  29.2 30.6 %all_gather.6 = bf16[64,192]{1,0:T(8,128)(2,1)S(1)} all-gather(bf16[8,192]{1,0:T(8,128)(2,1)S(1)} %convolution_convert_fusion), channel_id=1, replica_groups=mesh['ctx'=8,'grp'=4] {'ctx'}, dimensions={0}, use_global_device_ids=true | all-gather | bytes 27648 | tf_op jit(solution)/shard_map/all_gather | solution.py:67
  59.8 1.2 fusion.59
  63.7 3.9 %copy.68 = pred[8,256,1024]{1,2,0:T(32,128)(4,1)S(1)} copy(pred[8,256,1024]{2,1,0:T(8,128)(4,1)S(1)} %bitcast.98) | data formatting | bytes 4194304 | tf_op jit(solution)/shard_map/jit(_where)/broadcast_in_dim | solution.py:181
  67.6 1.4 gather_fusion
  69.0 1.3 gather_fusion.4
  71.5 2.5 %copy.73 = pred[2048,640]{0,1:T(32,128)(4,1)} copy(pred[2048,640]{1,0:T(8,128)(4,1)S(1)} %bitcast.100) | data formatting | bytes 2621440 | tf_op jit(solution)/shard_map/jit(_where)/broadcast_in_dim | solution.py:26
  75.5 1.5 fusion.28
  77.9 1.5 copy.62
  82.2 0.9 convolution_convert_fusion.1
  83.2 26.9 %all_gather.7 = bf16[64,128]{1,0:T(8,128)(2,1)} all-gather(bf16[8,128]{1,0:T(8,128)(2,1)S(1)} %convolution_convert_fusion.1), channel_id=1, replica_groups=mesh['ctx'=8,'grp'=4] {'ctx'}, dimensions={0}, use_global_device_ids=true | all-gather | bytes 18432 | tf_op jit(solution)/shard_map/all_gather | solution.py:68
  110.0 2.0 %copy.60 = bf16[2048,64]{1,0:T(8,128)(2,1)} copy(bf16[2048,64]{0,1:T(8,128)(2,1)} %get-tuple-element.17) | data formatting | bytes 524288 | tf_op jit(solution)/shard_map/convert_element_type | solution.py:98
  112.8 1.4 gather_fusion.1
  114.2 1.3 gather_fusion.5
  115.5 2.4 %reshape.570 = bf16[8,2,12288]{2,1,0:T(2,128)(2,1)} reshape(bf16[16,64,192]{2,1,0:T(8,128)(2,1)} %gather_fusion.1) | data formatting | bytes 786432 | tf_op jit(solution)/shard_map/reshape | solution.py:140
  117.9 1.7 reshape.576
  119.6 4.0 %all-to-all-start.2 = ((bf16[8,2,8192]{2,1,0:T(2,128)(2,1)}), bf16[8,2,8192]{2,1,0:T(2,128)(2,1)}, u32[]{:S(2)}, u32[]{:S(2)}) async-start(bf16[8,2,8192]{2,1,0:T(2,128)(2,1)} %reshape.576), calls=%async_computation.2 | async-start | bytes 524288 | tf_op jit(solution)/shard_map/all_to_all | solution.py:144
  124.6 0.9 constant_dynamic-update-slice_fusion.3
  125.5 0.9 constant_dynamic-update-slice_fusion.2
  126.4 0.9 constant_dynamic-update-slice_fusion.1
  128.1 4.7 %fusion.58 = (f32[2048]{0:T(1024)S(1)}, f32[2048,640]{0,1:T(8,128)}) fusion(pred[2048,640]{0,1:T(32,128)(4,1)} %copy.73, bf16[2048,192]{1,0:T(8,128)(2,1)S(1)} %reshape.567, bf16[640,320]{1,0:T(8,128)(2,1)S(1)} %constant_dynamic-update-slice_fusion), kind=kOutput, calls=%fused_computation.156 | convolution fusion | flops 507246592 | bytes 7938048 | tf_op jit(solution)/shard_map/dot_general | solution.py:22
  132.9 5.9 %all-to-all-start.1 = ((bf16[8,2,12288]{2,1,0:T(2,128)(2,1)}), bf16[8,2,12288]{2,1,0:T(2,128)(2,1)}, u32[]{:S(2)}, u32[]{:S(2)}) async-start(bf16[8,2,12288]{2,1,0:T(2,128)(2,1)} %reshape.570), calls=%async_computation.1 | async-start | bytes 786432 | tf_op jit(solution)/shard_map/all_to_all | solution.py:143
  138.8 4.8 %fusion.2 = (f32[2048]{0:T(1024)S(1)}, bf16[2048,640]{0,1:T(8,128)(2,1)}) fusion(f32[2048,640]{0,1:T(8,128)} %get-tuple-element.31, f32[2048]{0:T(1024)S(1)} %get-tuple-element.30), kind=kLoop, calls=%fused_computation.14 | loop fusion | flops 3930112 | bytes 7880704 | tf_op jit(solution)/shard_map/reduce_sum | solution.py:29
  143.6 4.4 %copy.74 = bf16[2048,640]{1,0:T(8,128)(2,1)} copy(bf16[2048,640]{0,1:T(8,128)(2,1)} %get-tuple-element.15) | data formatting | bytes 5242880 | tf_op jit(solution)/shard_map/convert_element_type | solution.py:30
  148.0 2.7 %fusion.22 = f32[128,16,128]{2,1,0:T(8,128)S(1)} fusion(bf16[128,16,640]{2,1,0:T(8,128)(2,1)} %bitcast.97, bf16[640,320]{1,0:T(8,128)(2,1)} %copy-done.8), kind=kOutput, calls=%fused_computation.48 | convolution fusion | flops 335544320 | bytes 3833856 | tf_op jit(solution)/shard_map/dot_general | solution.py:31
  150.6 1.4 copy.76
  152.2 1.2 reshape.577
  153.4 2.2 %gather_fusion.6 = bf16[120,64,128]{2,1,0:T(8,128)(2,1)} fusion(bf16[16,64,128]{2,1,0:T(8,128)(2,1)S(1)} %reshape.577, s32[1024]{0:T(1024)} %pad_clamp_fusion), kind=kCustom, calls=%fused_computation.6 | custom fusion | bytes 3932640 | tf_op jit(solution)/shard_map/gather | solution.py:147
  155.6 3.1 %pad_maximum_fusion.1 = bf16[8,16,64,128]{3,2,1,0:T(8,128)(2,1)} fusion(bf16[8,15,64,128]{3,2,1,0:T(8,128)(2,1)} %bitcast.99, bf16[8,1,64,128]{3,2,1,0:T(8,128)(2,1)S(1)} %bitcast.108), kind=kLoop, calls=%fused_computation.25 | loop fusion | flops 1048576 | bytes 4194304 | tf_op jit(solution)/shard_map/concatenate | solution.py:153
  158.7 1.5 reshape.571
  160.2 3.0 %gather_fusion.3 = bf16[120,64,192]{2,1,0:T(8,128)(2,1)} fusion(bf16[16,64,192]{2,1,0:T(8,128)(2,1)S(1)} %reshape.571, s32[1024]{0:T(1024)} %pad_clamp_fusion), kind=kCustom, calls=%fused_computation.3 | custom fusion | bytes 5898720 | tf_op jit(solution)/shard_map/gather | solution.py:146
  163.3 2.9 %pad_maximum_fusion = bf16[8,16,64,192]{3,2,1,0:T(8,128)(2,1)S(1)} fusion(bf16[8,15,64,192]{3,2,1,0:T(8,128)(2,1)} %bitcast.93, bf16[8,1,64,192]{3,2,1,0:T(8,128)(2,1)S(1)} %bitcast.105), kind=kLoop, calls=%fused_computation.18 | loop fusion | flops 1572864 | bytes 6291456 | tf_op jit(solution)/shard_map/concatenate | solution.py:149
  166.2 1.8 fusion.4
  168.0 3.2 %copy-done.1 = f32[8,1024,256]{2,1,0:T(8,128)} copy-done((f32[8,1024,256]{2,1,0:T(8,128)}, f32[8,1024,256]{2,1,0:T(8,128)S(1)}, u32[]{:S(2)}) %copy-start.1) | copy-done | bytes 8388632
  171.2 2.2 %fusion = f32[8,256]{1,0:T(8,128)S(1)} fusion(pred[8,256,1024]{1,2,0:T(32,128)(4,1)S(1)} %copy.68, f32[8,1024,256]{2,1,0:T(8,128)S(1)} %get-tuple-element.33, f32[8,256]{1,0:T(8,128)S(1)} %get-tuple-element.32), kind=kLoop, calls=%fused_computation.10 | loop fusion | flops 8386560 | bytes 10502144 | tf_op jit(solution)/shard_map/reduce_sum | solution.py:186
  173.6 7.6 %fusion.5 = f32[8,256,128]{2,1,0:T(8,128)} fusion(bf16[8,1024,128]{2,1,0:T(8,128)(2,1)} %bitcast.104, pred[8,256,1024]{1,2,0:T(32,128)(4,1)S(1)} %copy.68, f32[8,1024,256]{2,1,0:T(8,128)} %copy-done.1, f32[8,256]{1,0:T(8,128)S(1)} %get-tuple-element.32), kind=kOutput, calls=%fused_computation.17 | convolution fusion | flops 545259520 | bytes 13639680 | tf_op jit(solution)/shard_map/aqk,akd->aqd/dot_general | solution.py:187
  181.2 1.6 copy.71
  182.9 1.6 fusion.16
  184.5 1.0 copy.77
  (102 shorter events, 18.1 us)
Async XLA Ops:
  0.0 29.0 %copy-start = (bf16[192,192]{1,0:T(8,128)(2,1)S(1)}, bf16[192,192]{1,0:T(8,128)(2,1)}, u32[]{:S(2)}) copy-start(bf16[192,192]{1,0:T(8,128)(2,1)} %param.16) | copy-start | bytes 221188
  0.0 26.6 %copy-start.4 = (bf16[128,3072]{1,0:T(8,128)(2,1)S(1)}, bf16[128,3072]{1,0:T(8,128)(2,1)}, u32[]{:S(2)}) copy-start(bf16[128,3072]{1,0:T(8,128)(2,1)} %param.9) | copy-start | bytes 2359300
  0.0 28.8 %copy-start.10 = (bf16[32,192]{1,0:T(8,128)(2,1)S(1)}, bf16[32,192]{1,0:T(8,128)(2,1)}, u32[]{:S(2)}) copy-start(bf16[32,192]{1,0:T(8,128)(2,1)} %param.14) | copy-start | bytes 36868
  6.6 105.4 %all-to-all-start = ((s32[8,1,2]{2,1,0:T(1,128)}), s32[8,1,2]{2,1,0:T(1,128)}, u32[]{:S(2)}, u32[]{:S(2)}) async-start(s32[8,1,2]{2,1,0:T(1,128)} %bitcast.23), calls=%async_computation | async-start | bytes 8192 | tf_op jit(solution)/shard_map/all_to_all | solution.py:136
  17.2 106.5 %collective-permute-start = (bf16[128,320]{1,0:T(8,128)(2,1)}, bf16[128,320]{1,0:T(8,128)(2,1)}, u32[]{:S(2)}, u32[]{:S(2)}) collective-permute-start(bf16[128,320]{1,0:T(8,128)(2,1)} %get-tuple-element.20), channel_id=1, source_target_pairs={{0,16},{4,20},{8,24},{12,28},{16,0},{20,4},{24,8},{28,12},{1,17},{... | collective-permute-start | bytes 245768 | tf_op jit(solution)/shard_map/ppermute | solution.py:18
  20.1 104.5 %collective-permute-start.1 = (bf16[128,320]{1,0:T(8,128)(2,1)}, bf16[128,320]{1,0:T(8,128)(2,1)}, u32[]{:S(2)}, u32[]{:S(2)}) collective-permute-start(bf16[128,320]{1,0:T(8,128)(2,1)} %get-tuple-element.19), channel_id=1, source_target_pairs={{0,12},{4,16},{8,20},{12,24},{16,28},{20,0},{24,4},{28,8},{1,13},{... | collective-permute-start | bytes 245768 | tf_op jit(solution)/shard_map/ppermute | solution.py:18
  22.4 103.0 %collective-permute-start.2 = (bf16[128,320]{1,0:T(8,128)(2,1)}, bf16[128,320]{1,0:T(8,128)(2,1)}, u32[]{:S(2)}, u32[]{:S(2)}) collective-permute-start(bf16[128,320]{1,0:T(8,128)(2,1)} %get-tuple-element.18), channel_id=1, source_target_pairs={{0,8},{4,12},{8,16},{12,20},{16,24},{20,28},{24,0},{28,4},{1,9},{5... | collective-permute-start | bytes 245768 | tf_op jit(solution)/shard_map/ppermute | solution.py:18
  22.4 104.0 %collective-permute-start.3 = (bf16[128,320]{1,0:T(8,128)(2,1)}, bf16[128,320]{1,0:T(8,128)(2,1)}, u32[]{:S(2)}, u32[]{:S(2)}) collective-permute-start(bf16[128,320]{1,0:T(8,128)(2,1)} %get-tuple-element.11), channel_id=1, source_target_pairs={{0,4},{4,8},{8,12},{12,16},{16,20},{20,24},{24,28},{28,0},{1,5},{5... | collective-permute-start | bytes 245768 | tf_op jit(solution)/shard_map/ppermute | solution.py:18
  61.0 8.0 %copy-start.3 = (bf16[2,128,128]{2,1,0:T(8,128)(2,1)S(1)}, bf16[2,128,128]{2,1,0:T(8,128)(2,1)}, u32[]{:S(2)}) copy-start(bf16[2,128,128]{2,1,0:T(8,128)(2,1)} %param.11) | copy-start | bytes 196612
  70.3 3.7 %copy-start.5 = (f32[2048,64]{0,1:T(8,128)S(1)}, f32[2048,64]{0,1:T(8,128)}, u32[]{:S(2)}) copy-start(f32[2048,64]{0,1:T(8,128)} %get-tuple-element.35) | copy-start | bytes 1572868
  119.6 13.3 %all-to-all-start.2 = ((bf16[8,2,8192]{2,1,0:T(2,128)(2,1)}), bf16[8,2,8192]{2,1,0:T(2,128)(2,1)}, u32[]{:S(2)}, u32[]{:S(2)}) async-start(bf16[8,2,8192]{2,1,0:T(2,128)(2,1)} %reshape.576), calls=%async_computation.2 | async-start | bytes 524288 | tf_op jit(solution)/shard_map/all_to_all | solution.py:144
  127.4 0.8 copy-start.8
  132.9 25.8 %all-to-all-start.1 = ((bf16[8,2,12288]{2,1,0:T(2,128)(2,1)}), bf16[8,2,12288]{2,1,0:T(2,128)(2,1)}, u32[]{:S(2)}, u32[]{:S(2)}) async-start(bf16[8,2,12288]{2,1,0:T(2,128)(2,1)} %reshape.570), calls=%async_computation.1 | async-start | bytes 786432 | tf_op jit(solution)/shard_map/all_to_all | solution.py:143
  150.6 4.9 %copy-start.9 = (bf16[8,64,128]{2,1,0:T(8,128)(2,1)S(1)}, bf16[8,64,128]{2,1,0:T(8,128)(2,1)}, u32[]{:S(2)}) copy-start(bf16[8,64,128]{2,1,0:T(8,128)(2,1)} %gather_fusion.4) | copy-start | bytes 393220
  160.2 3.0 %copy-start.6 = (bf16[8,64,192]{2,1,0:T(8,128)(2,1)S(1)}, bf16[8,64,192]{2,1,0:T(8,128)(2,1)}, u32[]{:S(2)}) copy-start(bf16[8,64,192]{2,1,0:T(8,128)(2,1)} %gather_fusion) | copy-start | bytes 589828
  163.3 2.9 %copy-start.2 = (bf16[8,256,192]{2,1,0:T(8,128)(2,1)S(1)}, bf16[8,256,192]{2,1,0:T(8,128)(2,1)}, u32[]{:S(2)}) copy-start(bf16[8,256,192]{2,1,0:T(8,128)(2,1)} %reshape.574) | copy-start | bytes 2359300
  168.0 3.2 %copy-start.1 = (f32[8,1024,256]{2,1,0:T(8,128)}, f32[8,1024,256]{2,1,0:T(8,128)S(1)}, u32[]{:S(2)}) copy-start(f32[8,1024,256]{2,1,0:T(8,128)S(1)} %get-tuple-element.33) | copy-start | bytes 25165828
  173.6 9.3 %copy-start.7 = (f32[128,16,128]{0,2,1:T(8,128)S(1)}, f32[128,16,128]{0,2,1:T(8,128)}, u32[]{:S(2)}) copy-start(f32[128,16,128]{0,2,1:T(8,128)} %copy.76) | copy-start | bytes 3145732
  173.6 9.3 %copy-start.11 = (bf16[64,128]{1,0:T(8,128)(2,1)S(1)}, bf16[64,128]{1,0:T(8,128)(2,1)}, u32[]{:S(2)}) copy-start(bf16[64,128]{1,0:T(8,128)(2,1)} %all_gather.7) | copy-start | bytes 49156
  173.6 9.3 %copy-start.12 = (f32[128,16]{0,1:T(8,128)S(1)}, f32[128,16]{0,1:T(8,128)}, u32[]{:S(2)}) copy-start(f32[128,16]{0,1:T(8,128)} %copy.62) | copy-start | bytes 24580
  173.6 9.3 %copy-start.13 = (f32[128,16]{0,1:T(8,128)S(1)}, f32[128,16]{0,1:T(8,128)}, u32[]{:S(2)}) copy-start(f32[128,16]{0,1:T(8,128)} %get-tuple-element.23) | copy-start | bytes 24580
  173.6 9.3 %copy-start.14 = (f32[128,16]{0,1:T(8,128)S(1)}, f32[128,16]{0,1:T(8,128)}, u32[]{:S(2)}) copy-start(f32[128,16]{0,1:T(8,128)} %get-tuple-element.24) | copy-start | bytes 24580
  173.6 9.3 %copy-start.15 = (f32[128,16]{0,1:T(8,128)S(1)}, f32[128,16]{0,1:T(8,128)}, u32[]{:S(2)}) copy-start(f32[128,16]{0,1:T(8,128)} %get-tuple-element.25) | copy-start | bytes 24580
where the time goes:
time: 187 us; the launch traced here: 185 us
  local copies, waits for them, and re-layouts  57.5 us (31%)
  blocking collectives  57.5 us (31%)
  other arithmetic  25.6 us (14%)
  starting transfers between devices  23.6 us (13%)
  matrix products  20.8 us (11%)
    all_gather x1, blocking collectives, body(): lax.all_gather(comp_keys, 'ctx', axis=0, tiled=True)  30.6 us
    all_gather x1, blocking collectives, body(): lax.all_gather(comp_values, 'ctx', axis=0, tiled=True)  26.9 us
    unnamed x37, local copies, waits for them, and re-layouts  8.69 us
    dot_general x1, matrix products, body(): jnp.einsum('aqk,akd->aqd', weights.astype(jnp.bfloat16).reshape(groups, Q...  7.63 us
    all_to_all x1, starting transfers between devices, body(): lax.all_to_all(requests.reshape(devices, per_owner), 'ctx', split_axis=0,...  7.29 us
    ppermute x4, starting transfers between devices, shifted(): return lax.ppermute(value, axis, pairs)  6.41 us
    all_to_all x1, starting transfers between devices, body(): lax.all_to_all(out_keys, 'ctx', split_axis=0, concat_axis=0, tiled=True)  5.9 us
    reduce_sum x1, other arithmetic, attention(): totals = jnp.sum(weights, axis=2)  4.81 us
  transfers between devices with their start and end apart: 7, of which 0 were waited for; matrix products, arithmetic and copies ran while one was open for 38% of the time, Pallas kernels for 0%

commit v1 on v0

--- a/solution.py
+++ b/solution.py
@@ -1,6 +1,8 @@
 import jax
 import jax.numpy as jnp
 from jax import lax
+from jax.experimental import pallas as pl
+from jax.experimental.pallas import tpu as pltpu
 from jax.sharding import PartitionSpec as P
 
 HEADS = 16
@@ -32,7 +34,7 @@
     return mixture.reshape(-1, head_count, value_rows.shape[1]) / totals[:, :, None]
 
 
-def body(queries, keys, values, gate_logits, sel_ids, pos_k, pos_v, mix_k, mix_v):
+def exchange_body(queries, keys, values, gate_logits, sel_ids, pos_k, pos_v, mix_k, mix_v):
     devices = lax.axis_size("ctx")
     myself = lax.axis_index("ctx")
     rounds = keys.shape[0]
@@ -200,6 +202,281 @@
     return combined.reshape(tokens, HEADS * DV).astype(jnp.bfloat16)
 
 
+PAIR = 2
+COMP_ROWS = 48
+PIECE_ROWS = DK + DV
+CACHED_ROWS = PIECE_ROWS + COMP_ROWS
+HALF = 64
+STEP_HEADS = 4
+LOG2E = 1.4426950408889634
+
+
+def pack_kernel(keys_t, values, gains_k, gains_v, mix_k, mix_v, message):
+    rounds, _, tokens = keys_t.shape
+    count = tokens // CMP_BLOCK
+    pooled_k = jnp.zeros((DK, tokens), jnp.float32)
+    lane = lax.broadcasted_iota(jnp.int32, (tokens, tokens), 1)
+    segment = lax.broadcasted_iota(jnp.int32, (tokens, tokens), 0) // CMP_BLOCK
+    pooled_v = []
+    for piece in range(rounds):
+        base = 0 if piece == 0 else CACHED_ROWS
+        message[base : base + DK, :] = keys_t[piece]
+        message[base + DK : base + PIECE_ROWS, :] = values[piece]
+        product = keys_t[piece].astype(jnp.float32) * gains_k[...]
+        upper = product.astype(jnp.bfloat16)
+        lower = (product - upper.astype(jnp.float32)).astype(jnp.bfloat16)
+        picks = (lane == segment + piece * count).astype(jnp.bfloat16)
+        pooled_k += jnp.dot(upper, picks, preferred_element_type=jnp.float32)
+        pooled_k += jnp.dot(lower, picks, preferred_element_type=jnp.float32)
+        product_v = values[piece].astype(jnp.float32) * gains_v[...]
+        pooled_v.append(jnp.sum(product_v.reshape(count, CMP_BLOCK, DV), axis=1))
+    comp_k = lax.dot_general(
+        pooled_k.astype(jnp.bfloat16),
+        mix_k[...],
+        (((0,), (0,)), ((), ())),
+        preferred_element_type=jnp.float32,
+    )[: rounds * count]
+    comp_v = jnp.dot(
+        jnp.concatenate(pooled_v, axis=0).astype(jnp.bfloat16),
+        mix_v[...],
+        preferred_element_type=jnp.float32,
+    )
+    gap = jnp.zeros((rounds * count, HALF), jnp.float32)
+    low = jnp.concatenate([comp_k, gap], axis=1)
+    high = jnp.concatenate([gap, comp_k], axis=1)
+    rows = [low[:, :DV], low[:, DV:], high[:, :DV], high[:, DV:], comp_v]
+    rows.append(jnp.zeros((COMP_ROWS - 5 * rounds * count, DV), jnp.float32))
+    message[PIECE_ROWS:CACHED_ROWS, :] = jnp.concatenate(rows, axis=0).astype(jnp.bfloat16)
+
+
+def softmax_parts(scores):
+    highest = scores[0].max(axis=1, keepdims=True)
+    for part in scores[1:]:
+        highest = jnp.maximum(highest, part.max(axis=1, keepdims=True))
+    factor = DK ** (-0.5) * LOG2E
+    return [jnp.exp2((part - highest) * factor).astype(jnp.bfloat16) for part in scores]
+
+
+def weighted(weights, values):
+    mixed = jnp.dot(weights[0], values[0], preferred_element_type=jnp.float32)
+    for weight, value in zip(weights[1:], values[1:]):
+        mixed += jnp.dot(weight, value, preferred_element_type=jnp.float32)
+    return mixed[:, :DV] / mixed[:, DV:]
+
+
+def attend_kernel(
+    where_from,
+    queries,
+    gates,
+    sel_bias,
+    cmp_bias,
+    *rest,
+):
+    *messages, output, far_low, far_high, far_values, near_low, near_high, near_values = rest[:-4]
+    comp_low, comp_high, comp_values, bias = rest[-4:]
+    tokens = queries.shape[0]
+    slots = len(messages)
+    per_slot = 2 * tokens // CMP_BLOCK
+
+    @pl.when(pl.program_id(0) == 0)
+    def _():
+        for low, high in ((far_low, far_high), (near_low, near_high)):
+            nothing = jnp.zeros((HALF, low.shape[1]), jnp.bfloat16)
+            low[DK:, :] = nothing
+            high[:HALF, :] = nothing
+        for ref in (far_values, near_values, comp_values):
+            ref[:, DV:] = jnp.ones((ref.shape[0], DV), jnp.bfloat16)
+        for slot, message in enumerate(messages):
+            span = slice(slot * tokens, (slot + 1) * tokens)
+            far_low[:DK, span] = message[:DK, :]
+            far_high[HALF:, span] = message[:DK, :]
+            far_values[span, :DV] = message[DK:PIECE_ROWS, :]
+            rows = slice(slot * per_slot, (slot + 1) * per_slot)
+            part = message[PIECE_ROWS:CACHED_ROWS, :].astype(jnp.float32)
+            comp_low[rows, :DV] = part[:per_slot]
+            comp_low[rows, DV:] = part[per_slot : 2 * per_slot]
+            comp_high[rows, :DV] = part[2 * per_slot : 3 * per_slot]
+            comp_high[rows, DV:] = part[3 * per_slot : 4 * per_slot]
+            comp_values[rows, :DV] = part[4 * per_slot : 5 * per_slot].astype(jnp.bfloat16)
+        for place in range(5):
+            lanes = slice(place * tokens, (place + 1) * tokens)
+
+            def fetch(message, start):
+                part = message[pl.ds(start, PIECE_ROWS), :]
+                near_low[:DK, lanes] = part[:DK]
+                near_high[HALF:, lanes] = part[:DK]
+                near_values[lanes, :DV] = part[DK:]
+
+            if place == 4:
+                fetch(messages[0], CACHED_ROWS)
+                continue
+            for slot, message in enumerate(messages):
+
+                @pl.when(where_from[0, place] == slot)
+                def _():
+                    start = where_from[1, place] * CACHED_ROWS
+                    fetch(message, pl.multiple_of(start, 16))
+
+        groups = sel_bias.shape[0]
+        width = sel_bias.shape[1]
+        bias[...] = jnp.broadcast_to(
+            sel_bias[...][:, None, :], (groups, tokens // groups, width)
+        ).reshape(tokens, width)
+
+    query = lax.broadcasted_iota(jnp.int32, (tokens, tokens), 0)
+    place_at = lax.broadcasted_iota(jnp.int32, (tokens, tokens), 1)
+    never = jnp.float32(-jnp.inf)
+    causal = jnp.where(place_at <= query, 0.0, never)
+    expiring = jnp.where(place_at > query, 0.0, never)
+    own_block = jnp.where(
+        (place_at <= query) & (place_at // SEL_BLOCK == query // SEL_BLOCK), 0.0, never
+    )
+
+    def add(scores, mask):
+        width = scores.shape[1]
+        shape = (scores.shape[0] // tokens, tokens, width)
+        return (scores.reshape(shape) + mask[None]).reshape(scores.shape)
+
+    gate = jax.nn.sigmoid(gates[0].astype(jnp.float32))
+    for odd, far, near, comp in ((0, far_low, near_low, comp_low), (1, far_high, near_high, comp_high)):
+        first = odd * DV
+        stride = 2 * DK
+        rows = jnp.concatenate(
+            [queries[:, first : first + 2 * DV], queries[:, first + stride : first + stride + 2 * DV]],
+            axis=0,
+        )
+        near_scores = jnp.dot(rows, near[...], preferred_element_type=jnp.float32)
+        far_scores = jnp.dot(rows, far[...], preferred_element_type=jnp.float32)
+        comp_scores = lax.dot_general(
+            rows,
+            comp[...].astype(jnp.bfloat16),
+            (((1,), (1,)), ((), ())),
+            preferred_element_type=jnp.float32,
+        )
+        own = near_scores[:, 4 * tokens :]
+        sliding = weighted(
+            softmax_parts(
+                [
+                    add(near_scores[:, :tokens], expiring),
+                    near_scores[:, tokens : 4 * tokens],
+                    add(own, causal),
+                ]
+            ),
+            [
+                near_values[:tokens, :],
+                near_values[tokens : 4 * tokens, :],
+                near_values[4 * tokens :, :],
+            ],
+        )
+        selected = weighted(
+            softmax_parts([add(far_scores, bias[...]), add(own, own_block)]),
+            [far_values[...], near_values[4 * tokens :, :]],
+        )
+        compressed = weighted(softmax_parts([add(comp_scores, cmp_bias[...])]), [comp_values[...]])
+        for which in range(2):
+            head = 2 * which + odd
+            at = slice(which * tokens, (which + 1) * tokens)
+            total = (
+                gate[:, head : head + 1] * compressed[at]
+                + gate[:, STEP_HEADS + head : STEP_HEADS + head + 1] * selected[at]
+                + gate[:, 2 * STEP_HEADS + head : 2 * STEP_HEADS + head + 1] * sliding[at]
+            )
+            output[:, head * DV : (head + 1) * DV] = total.astype(jnp.bfloat16)
+
+
+def dense_body(queries, keys, values, gate_logits, sel_ids, pos_k, pos_v, mix_k, mix_v):
+    devices = lax.axis_size("ctx")
+    myself = lax.axis_index("ctx")
+    tokens = keys.shape[1]
+    groups = sel_ids.shape[0]
+    majors = devices // PAIR
+    repeat = tokens // CMP_BLOCK
+    gains_k = jnp.tile(pos_k.T.astype(jnp.float32), (1, repeat))
+    gains_v = jnp.tile(pos_v.astype(jnp.float32), (repeat, 1))
+    rows = CACHED_ROWS + PIECE_ROWS
+    message = pl.pallas_call(
+        pack_kernel,
+        out_shape=jax.ShapeDtypeStruct((rows, tokens), jnp.bfloat16),
+        name="pack",
+    )(jnp.swapaxes(keys, 1, 2), values, gains_k, gains_v, mix_k, mix_v)
+
+    def flipped(value):
+        return lax.ppermute(value, "ctx", [(i, i ^ 1) for i in range(devices)])
+
+    moved = []
+    for step in range(1, majors):
+        sent = message if step <= 2 else message[:CACHED_ROWS]
+        moved.append(shifted(sent, "ctx", step * PAIR))
+    other = flipped(message)
+    messages = [message, other]
+    for value in moved:
+        messages += [value, flipped(value)]
+    major, side = myself // PAIR, myself % PAIR
+    holders = []
+    for step in range(majors):
+        source = (major - step) % majors * PAIR
+        holders += [source + side, source + 1 - side]
+    holders = jnp.stack(holders).astype(jnp.int32)
+    distance = jnp.array([4, 3, 2, 1], jnp.int32)
+    piece = myself - distance
+    slot = jnp.where(side == 0, jnp.array([4, 5, 2, 3]), jnp.array([4, 3, 2, 1]))
+    where_from = jnp.stack([slot, (piece >= 0).astype(jnp.int32)]).astype(jnp.int32)
+    per_block = tokens // SEL_BLOCK
+    block_of = (holders[:, None] * per_block + jnp.arange(per_block, dtype=jnp.int32)).reshape(-1)
+    named = jnp.any(sel_ids[:, 1:, None] == block_of[None, None, :], axis=1)
+    sel_bias = jnp.repeat(jnp.where(named, 0.0, -jnp.inf), SEL_BLOCK, axis=1)
+    offset = jnp.arange(tokens, dtype=jnp.int32)[:, None]
+    ends = (jnp.arange(repeat, dtype=jnp.int32) + 1) * CMP_BLOCK - 1
+    ready = jnp.where(holders[:, None] == myself, ends[None, :], jnp.where(holders[:, None] < myself, -1, tokens))
+    ready = jnp.concatenate([jnp.full((devices, repeat), -1, jnp.int32), ready], axis=1).reshape(-1)
+    cmp_bias = jnp.where(ready[None, :] <= offset, 0.0, -jnp.inf)
+    steps = HEADS // STEP_HEADS
+    gates = (
+        gate_logits.reshape(tokens, 3, steps, STEP_HEADS)
+        .transpose(2, 0, 1, 3)
+        .reshape(steps, tokens, 3 * STEP_HEADS)
+    )
+    far = devices * tokens
+    comps = devices * 2 * repeat
+    whole = lambda value: pl.BlockSpec(value.shape, lambda i: (0,) * value.ndim)
+    return pl.pallas_call(
+        attend_kernel,
+        grid=(steps,),
+        in_specs=[
+            pl.BlockSpec(memory_space=pltpu.SMEM),
+            pl.BlockSpec((tokens, STEP_HEADS * DK), lambda i: (0, i)),
+            pl.BlockSpec((1, tokens, 3 * STEP_HEADS), lambda i: (i, 0, 0)),
+            whole(sel_bias),
+            whole(cmp_bias),
+        ]
+        + [whole(value) for value in messages],
+        out_specs=pl.BlockSpec((tokens, STEP_HEADS * DV), lambda i: (0, i)),
+        out_shape=jax.ShapeDtypeStruct((tokens, HEADS * DV), jnp.bfloat16),
+        scratch_shapes=[
+            pltpu.VMEM((2 * DV, far), jnp.bfloat16),
+            pltpu.VMEM((2 * DV, far), jnp.bfloat16),
+            pltpu.VMEM((far, 2 * DV), jnp.bfloat16),
+            pltpu.VMEM((2 * DV, 5 * tokens), jnp.bfloat16),
+            pltpu.VMEM((2 * DV, 5 * tokens), jnp.bfloat16),
+            pltpu.VMEM((5 * tokens, 2 * DV), jnp.bfloat16),
+            pltpu.VMEM((comps, 2 * DV), jnp.float32),
+            pltpu.VMEM((comps, 2 * DV), jnp.float32),
+            pltpu.VMEM((comps, 2 * DV), jnp.bfloat16),
+            pltpu.VMEM((tokens, far), jnp.float32),
+        ],
+        name="attend",
+    )(where_from, queries, gates, sel_bias, cmp_bias, *messages)
+
+
+def body(queries, keys, *others):
+    devices = lax.axis_size("ctx")
+    rounds, tokens = keys.shape[:2]
+    blocks = (rounds - 1) * tokens // SEL_BLOCK * devices
+    dense = rounds == 2 and blocks <= SPREAD and devices % PAIR == 0 and devices >= 6
+    chosen = dense_body if dense else exchange_body
+    return chosen(queries, keys, *others)
+
+
 def solution(mesh):
     in_specs = (
         P("ctx", "grp"),

time: 187 us -> 44.2 us (0.24)
  blocking collectives: 57.5 us -> 0 us
  local copies, waits for them, and re-layouts: 57.5 us -> 6.25 us
  other arithmetic: 25.6 us -> 2.21 us
  matrix products: 20.8 us -> 0 us
  Pallas kernels: 0 us -> 12.6 us
  starting transfers between devices: 23.6 us -> 13.1 us
  waiting for transfers between devices: 0.02 us -> 9.52 us
    all_gather x2 -> x0, blocking collectives: 57.5 us -> none  [the longest x1 30.6 us: body(): lax.all_gather(comp_keys, 'ctx', axis=0, tiled=True)]
    dot_general x8 -> x0, matrix products: 20.8 us -> none  [the longest x1 7.63 us: body(): jnp.einsum('aqk,akd->aqd', weights.astype(jnp.bfloat16).reshape(groups, Q...]
    all_to_all x3 -> x0, starting transfers between devices: 17.2 us -> none  [the longest x1 7.29 us: body(): lax.all_to_all(requests.reshape(devices, per_owner), 'ctx', split_axis=0,...]
    pallas_call x0 -> x2, Pallas kernels: none -> 12.6 us  [the longest x1 10.4 us: dense_body(): pl.pallas_call(attend_kernel, grid=(steps,), in_specs=[pl.BlockSpec(memor...]
    gather x7 -> x0, local copies, waits for them, and re-layouts: 11.8 us -> none  [the longest x1 3.03 us: body(): near_keys = got_keys.reshape(devices * per_owner, SEL_BLOCK, DK)[fetch_at]]
    reshape x7 -> x3, local copies, waits for them, and re-layouts: 12.6 us -> 1.5 us  [the longest x1 0.79 us: dense_body(): gates = gate_logits.reshape(tokens, 3, steps, STEP_HEADS).transpose(2, 0,...]
    broadcast_in_dim x9 -> x1, local copies, waits for them, and re-layouts: 8.07 us -> 0.07 us  [dense_body(): sel_bias = jnp.repeat(jnp.where(named, 0.0, -jnp.inf), SEL_BLOCK, axis=1)]
    reduce_sum x4 -> x0, other arithmetic: 7.97 us -> none  [the longest x1 4.81 us: attention(): totals = jnp.sum(weights, axis=2)]
  transfers between devices with their start and end apart: 7 -> 7, of which waited for: 0 -> 2; matrix products, arithmetic and copies ran while one was open for 38% -> 10% of each run, Pallas kernels for 0% -> 0%
where the time goes in v1:
time: 44.2 us; the launch traced here: 43.8 us
  starting transfers between devices  13.1 us (30%)
  Pallas kernels  12.6 us (29%)
  waiting for transfers between devices  9.52 us (22%)
  local copies, waits for them, and re-layouts  6.25 us (14%)
  other arithmetic  2.21 us (5%)
    pallas_call x1, Pallas kernels, dense_body(): pl.pallas_call(attend_kernel, grid=(steps,), in_specs=[pl.BlockSpec(memor...  10.4 us
    ppermute x3, starting transfers between devices, shifted(): return lax.ppermute(value, axis, pairs)  7.89 us
    ppermute x4, starting transfers between devices, flipped(): return lax.ppermute(value, 'ctx', [(i, i ^ 1) for i in range(devices)])  5.22 us
    ppermute x3, waiting for transfers between devices, shifted(): return lax.ppermute(value, axis, pairs)  4.88 us
    ppermute x4, waiting for transfers between devices, flipped(): return lax.ppermute(value, 'ctx', [(i, i ^ 1) for i in range(devices)])  4.63 us
    pallas_call x1, Pallas kernels, dense_body(): pl.pallas_call(pack_kernel, out_shape=jax.ShapeDtypeStruct((rows, tokens)...  2.19 us
    unnamed x26, local copies, waits for them, and re-layouts  1.89 us
    slice x1, local copies, waits for them, and re-layouts, dense_body(): sent = message if step <= 2 else message[:CACHED_ROWS]  0.93 us
  transfers between devices with their start and end apart: 7, of which 2 were waited for; matrix products, arithmetic and copies ran while one was open for 10% of the time, Pallas kernels for 0%

profile of v1, /device:TPU:0, one launch (start us, length us, event | category | flops | bytes accessed | tf_op | source)
XLA Modules:
  0.0 43.8 jit_solution(5314692581492058504)
XLA Ops:
  0.0 0.7 %convert_bitcast_fusion = f32[192,32]{0,1:T(8,128)S(1)} fusion(bf16[32,192]{1,0:T(8,128)(2,1)} %param.17), kind=kLoop, calls=%fused_computation.3 | loop fusion | flops 6144 | bytes 36864 | tf_op jit(solution)/shard_map/convert_element_type | solution.py:394
  0.7 0.0 copy-start.8
  0.7 0.7 %copy.20.gains_k = f32[192,128]{1,0:T(8,128)} copy(f32[192,128]{0,1:T(8,128)S(1)} %bitcast.21) | data formatting | bytes 196608 | tf_op jit(solution)/shard_map/tile | solution.py:394
  1.5 0.0 copy-done.8
  1.5 0.6 %tile.20 = f32[4,32,128]{2,1,0:T(8,128)} broadcast(bf16[32,128]{1,0:T(8,128)(2,1)S(1)} %copy-done.8), dimensions={1,2} | broadcast | bytes 73728 | tf_op jit(solution)/shard_map/tile | solution.py:395
  2.1 2.2 %pack.1.rest_0_ = bf16[688,128]{1,0:T(8,128)(2,1)} custom-call(bf16[2,192,128]{2,1,0:T(8,128)(2,1)} %bitcast.23, bf16[2,128,128]{2,1,0:T(8,128)(2,1)} %values.1, f32[192,128]{1,0:T(8,128)} %copy.20.gains_k, f32[128,128]{1,0:T(8,128)} %bitcast.22, bf16[192,192]{1,0:T(8,128)(2,1)} %mix_k.1, bf16[128,128]{1,0:T(8,128)(2,1)} %mix_v.1), custom_call_target="tpu_custom_call" | custom-call | tf_op jit(solution)/shard_map/pack/pallas_call | solution.py:397
  4.3 4.1 %collective-permute-start.3 = (bf16[688,128]{1,0:T(8,128)(2,1)}, bf16[688,128]{1,0:T(8,128)(2,1)S(1)}, u32[]{:S(2)}, u32[]{:S(2)}) collective-permute-start(bf16[688,128]{1,0:T(8,128)(2,1)} %pack.1.rest_0_), channel_id=1, source_target_pairs={{0,16},{4,20},{8,24},{12,28},{16,0},{20,4},{24,8},{28,12},{1,17},{... | collective-permute-start | bytes 528392 | tf_op jit(solution)/shard_map/ppermute | solution.py:20
  8.4 1.6 %collective-permute-start.1 = (bf16[688,128]{1,0:T(8,128)(2,1)}, bf16[688,128]{1,0:T(8,128)(2,1)S(1)}, u32[]{:S(2)}, u32[]{:S(2)}) collective-permute-start(bf16[688,128]{1,0:T(8,128)(2,1)} %pack.1.rest_0_), channel_id=1, source_target_pairs={{0,8},{4,12},{8,16},{12,20},{16,24},{20,28},{24,0},{28,4},{1,9},{5... | collective-permute-start | bytes 528392 | tf_op jit(solution)/shard_map/ppermute | solution.py:20
  9.9 1.5 %collective-permute-start = (bf16[688,128]{1,0:T(8,128)(2,1)}, bf16[688,128]{1,0:T(8,128)(2,1)S(1)}, u32[]{:S(2)}, u32[]{:S(2)}) collective-permute-start(bf16[688,128]{1,0:T(8,128)(2,1)} %pack.1.rest_0_), channel_id=1, source_target_pairs={{0,4},{4,0},{8,12},{12,8},{16,20},{20,16},{24,28},{28,24},{1,5},{5... | collective-permute-start | bytes 528392 | tf_op jit(solution)/shard_map/ppermute | solution.py:404
  11.4 0.9 %slice.8 = bf16[368,128]{1,0:T(8,128)(2,1)S(1)} slice(bf16[688,128]{1,0:T(8,128)(2,1)} %pack.1.rest_0_), slice={[0:368], [0:128]} | slice | bytes 188416 | tf_op jit(solution)/shard_map/slice | solution.py:408
  12.4 2.2 %collective-permute-start.5 = (bf16[368,128]{1,0:T(8,128)(2,1)S(1)}, bf16[368,128]{1,0:T(8,128)(2,1)S(1)}, u32[]{:S(2)}, u32[]{:S(2)}) collective-permute-start(bf16[368,128]{1,0:T(8,128)(2,1)S(1)} %slice.8), channel_id=1, source_target_pairs={{0,24},{4,28},{8,0},{12,4},{16,8},{20,12},{24,16},{28,20},{1,25},{... | collective-permute-start | bytes 282632 | tf_op jit(solution)/shard_map/ppermute | solution.py:20
  14.6 0.1 stack.51
  14.7 0.1 broadcast_select_fusion
  14.8 0.1 concatenate.15
  14.9 0.1 le.15
  15.0 0.1 iota_add_fusion
  15.0 0.1 add.94
  15.1 0.5 %copy-done.9 = s32[8,16]{1,0:T(8,128)S(1)} copy-done((s32[8,16]{1,0:T(8,128)S(1)}, s32[8,16]{1,0:T(8,128)}, u32[]{:S(2)}) %copy-start.9) | copy-done | bytes 536
  15.7 0.1 slice.6
  15.7 0.1 copy.19
  15.8 0.1 compare_reduce_fusion
  15.9 0.0 copy-start.10
  15.9 0.0 copy-start.11
  15.9 0.0 copy-start.7
  16.0 0.6 %fusion.cmp_bias = f32[128,64]{1,0:T(8,128)} fusion(s32[64]{0:T(128)S(1)} %le.15), kind=kLoop, calls=%fused_computation.1 | loop fusion | flops 16384 | bytes 33024 | tf_op jit(solution)/shard_map/jit(_where)/select_n | solution.py:432
  16.6 0.0 copy-done.10
  16.6 0.0 copy-done.11
  16.6 4.9 %collective-permute-done.3.rest_4_ = bf16[688,128]{1,0:T(8,128)(2,1)S(1)} collective-permute-done((bf16[688,128]{1,0:T(8,128)(2,1)}, bf16[688,128]{1,0:T(8,128)(2,1)S(1)}, u32[]{:S(2)}, u32[]{:S(2)}) %collective-permute-start.3) | collective-permute-done | bytes 176160 | tf_op jit(solution)/shard_map/ppermute | solution.py:20
  21.5 1.7 %collective-permute-start.4 = (bf16[688,128]{1,0:T(8,128)(2,1)S(1)}, bf16[688,128]{1,0:T(8,128)(2,1)S(1)}, u32[]{:S(2)}, u32[]{:S(2)}) collective-permute-start(bf16[688,128]{1,0:T(8,128)(2,1)S(1)} %collective-permute-done.3.rest_4_), channel_id=1, source_target_pairs={{0,4},{4,0},{8,12},{12,8},{16,20},{20,16},{24,28},{28,24},{1,5},{5... | collective-permute-start | bytes 528392 | tf_op jit(solution)/shard_map/ppermute | solution.py:404
  23.2 0.0 collective-permute-done.1.rest_2_
  23.2 0.3 collective-permute-start.2
  23.5 0.0 copy-done.12
  23.5 0.0 copy-done.7
  23.5 0.1 broadcast_in_dim.61
  23.6 0.7 %reshape.241.sel_bias = f32[8,1024]{1,0:T(8,128)} reshape(f32[8,16,64]{2,1,0:T(8,128)S(1)} %broadcast_in_dim.61) | data formatting | bytes 65536 | tf_op jit(solution)/shard_map/reshape | solution.py:427
  24.3 0.8 %copy.21.gates = bf16[4,128,12]{2,1,0:T(8,128)(2,1)} copy(bf16[4,128,12]{1,0,2:T(4,128)(2,1)S(1)} %bitcast.24) | data formatting | bytes 24576 | tf_op jit(solution)/shard_map/reshape | solution.py:437
  25.1 0.0 collective-permute-done.5.rest_6_
  25.1 1.7 %collective-permute-start.6 = (bf16[368,128]{1,0:T(8,128)(2,1)S(1)}, bf16[368,128]{1,0:T(8,128)(2,1)S(1)}, u32[]{:S(2)}, u32[]{:S(2)}) collective-permute-start(bf16[368,128]{1,0:T(8,128)(2,1)S(1)} %collective-permute-done.5.rest_6_), channel_id=1, source_target_pairs={{0,4},{4,0},{8,12},{12,8},{16,20},{20,16},{24,28},{28,24},{1,5},{5... | collective-permute-start | bytes 282632 | tf_op jit(solution)/shard_map/ppermute | solution.py:404
  26.8 0.6 %pad_add_fusion.where_from = s32[2,4]{1,0:T(2,128)} fusion(s32[1,4]{1,0:T(1,128)S(1)} %fusion.2, s32[1,4]{1,0:T(1,128)S(1)} %fusion.1), kind=kLoop, calls=%fused_computation.9 | loop fusion | flops 8 | bytes 64 | tf_op jit(solution)/shard_map/stack | solution.py:423
  27.4 0.0 collective-permute-done.rest_1_
  27.4 4.6 %collective-permute-done.6.rest_7_ = bf16[368,128]{1,0:T(8,128)(2,1)S(1)} collective-permute-done((bf16[368,128]{1,0:T(8,128)(2,1)S(1)}, bf16[368,128]{1,0:T(8,128)(2,1)S(1)}, u32[]{:S(2)}, u32[]{:S(2)}) %collective-permute-start.6) | collective-permute-done | bytes 94240 | tf_op jit(solution)/shard_map/ppermute | solution.py:404
  32.1 0.0 collective-permute-done.4.rest_5_
  32.1 0.0 collective-permute-done.2.rest_3_
  32.1 0.0 copy-done
  32.1 0.6 %copy-done.6 = bf16[368,128]{1,0:T(8,128)(2,1)} copy-done((bf16[368,128]{1,0:T(8,128)(2,1)}, bf16[368,128]{1,0:T(8,128)(2,1)S(1)}, u32[]{:S(2)}) %copy-start.6) | copy-done | bytes 94232
  32.7 0.1 copy-done.3
  32.7 0.7 %copy-done.4 = bf16[688,128]{1,0:T(8,128)(2,1)} copy-done((bf16[688,128]{1,0:T(8,128)(2,1)}, bf16[688,128]{1,0:T(8,128)(2,1)S(1)}, u32[]{:S(2)}) %copy-start.4) | copy-done | bytes 176152
  33.4 10.4 %attend.1 = bf16[128,2048]{1,0:T(8,128)(2,1)} custom-call(s32[2,4]{1,0:T(2,128)} %pad_add_fusion.where_from, bf16[128,3072]{1,0:T(8,128)(2,1)} %queries.1, bf16[4,128,12]{2,1,0:T(8,128)(2,1)} %copy.21.gates, f32[8,1024]{1,0:T(8,128)} %reshape.241.sel_bias, f32[128,64]{1,0:T(8,128)} %fusion.cmp_bias, bf16[688,128]{1,0:T(8,128)(2,1)} %pack.1.rest_0_, ...), custom_call_target="tpu_custom_call" | custom-call | tf_op jit(solution)/shard_map/attend/pallas_call | solution.py:442
  (20 shorter events, 0.1 us)
Async XLA Ops:
  0.7 0.8 %copy-start.8 = (bf16[32,128]{1,0:T(8,128)(2,1)S(1)}, bf16[32,128]{1,0:T(8,128)(2,1)}, u32[]{:S(2)}) copy-start(bf16[32,128]{1,0:T(8,128)(2,1)} %param.18) | copy-start | bytes 24580
  4.3 17.2 %collective-permute-start.3 = (bf16[688,128]{1,0:T(8,128)(2,1)}, bf16[688,128]{1,0:T(8,128)(2,1)S(1)}, u32[]{:S(2)}, u32[]{:S(2)}) collective-permute-start(bf16[688,128]{1,0:T(8,128)(2,1)} %pack.1.rest_0_), channel_id=1, source_target_pairs={{0,16},{4,20},{8,24},{12,28},{16,0},{20,4},{24,8},{28,12},{1,17},{... | collective-permute-start | bytes 528392 | tf_op jit(solution)/shard_map/ppermute | solution.py:20
  8.4 14.8 %collective-permute-start.1 = (bf16[688,128]{1,0:T(8,128)(2,1)}, bf16[688,128]{1,0:T(8,128)(2,1)S(1)}, u32[]{:S(2)}, u32[]{:S(2)}) collective-permute-start(bf16[688,128]{1,0:T(8,128)(2,1)} %pack.1.rest_0_), channel_id=1, source_target_pairs={{0,8},{4,12},{8,16},{12,20},{16,24},{20,28},{24,0},{28,4},{1,9},{5... | collective-permute-start | bytes 528392 | tf_op jit(solution)/shard_map/ppermute | solution.py:20
  9.9 17.5 %collective-permute-start = (bf16[688,128]{1,0:T(8,128)(2,1)}, bf16[688,128]{1,0:T(8,128)(2,1)S(1)}, u32[]{:S(2)}, u32[]{:S(2)}) collective-permute-start(bf16[688,128]{1,0:T(8,128)(2,1)} %pack.1.rest_0_), channel_id=1, source_target_pairs={{0,4},{4,0},{8,12},{12,8},{16,20},{20,16},{24,28},{28,24},{1,5},{5... | collective-permute-start | bytes 528392 | tf_op jit(solution)/shard_map/ppermute | solution.py:404
  12.4 12.8 %collective-permute-start.5 = (bf16[368,128]{1,0:T(8,128)(2,1)S(1)}, bf16[368,128]{1,0:T(8,128)(2,1)S(1)}, u32[]{:S(2)}, u32[]{:S(2)}) collective-permute-start(bf16[368,128]{1,0:T(8,128)(2,1)S(1)} %slice.8), channel_id=1, source_target_pairs={{0,24},{4,28},{8,0},{12,4},{16,8},{20,12},{24,16},{28,20},{1,25},{... | collective-permute-start | bytes 282632 | tf_op jit(solution)/shard_map/ppermute | solution.py:20
  15.0 0.7 %copy-start.9 = (s32[8,16]{1,0:T(8,128)S(1)}, s32[8,16]{1,0:T(8,128)}, u32[]{:S(2)}) copy-start(s32[8,16]{1,0:T(8,128)} %param.16) | copy-start | bytes 1540
  15.9 0.7 %copy-start.10 = (s32[4]{0:T(128)S(1)}, s32[4]{0:T(128)}, u32[]{:S(2)}) copy-start(s32[4]{0:T(128)} %constant.81.clone) | copy-start | bytes 52
  15.9 0.7 %copy-start.11 = (s32[4]{0:T(128)S(1)}, s32[4]{0:T(128)}, u32[]{:S(2)}) copy-start(s32[4]{0:T(128)} %constant.80.clone) | copy-start | bytes 52
  15.9 7.6 %copy-start.7 = (bf16[128,48]{0,1:T(8,128)(2,1)S(1)}, bf16[128,48]{0,1:T(8,128)(2,1)}, u32[]{:S(2)}) copy-start(bf16[128,48]{0,1:T(8,128)(2,1)} %param.15) | copy-start | bytes 36868
  16.6 6.9 %copy-start.12 = (s32[4]{0:T(128)S(1)}, s32[4]{0:T(128)}, u32[]{:S(2)}) copy-start(s32[4]{0:T(128)} %constant.84) | copy-start | bytes 52
  21.5 10.6 %copy-start = (bf16[688,128]{1,0:T(8,128)(2,1)}, bf16[688,128]{1,0:T(8,128)(2,1)S(1)}, u32[]{:S(2)}) copy-start(bf16[688,128]{1,0:T(8,128)(2,1)S(1)} %collective-permute-done.3.rest_4_) | copy-start | bytes 528388
  21.5 10.6 %collective-permute-start.4 = (bf16[688,128]{1,0:T(8,128)(2,1)S(1)}, bf16[688,128]{1,0:T(8,128)(2,1)S(1)}, u32[]{:S(2)}, u32[]{:S(2)}) collective-permute-start(bf16[688,128]{1,0:T(8,128)(2,1)S(1)} %collective-permute-done.3.rest_4_), channel_id=1, source_target_pairs={{0,4},{4,0},{8,12},{12,8},{16,20},{20,16},{24,28},{28,24},{1,5},{5... | collective-permute-start | bytes 528392 | tf_op jit(solution)/shard_map/ppermute | solution.py:404
  23.2 8.9 %copy-start.1 = (bf16[688,128]{1,0:T(8,128)(2,1)}, bf16[688,128]{1,0:T(8,128)(2,1)S(1)}, u32[]{:S(2)}) copy-start(bf16[688,128]{1,0:T(8,128)(2,1)S(1)} %collective-permute-done.1.rest_2_) | copy-start | bytes 528388
  23.2 8.9 %collective-permute-start.2 = (bf16[688,128]{1,0:T(8,128)(2,1)S(1)}, bf16[688,128]{1,0:T(8,128)(2,1)S(1)}, u32[]{:S(2)}, u32[]{:S(2)}) collective-permute-start(bf16[688,128]{1,0:T(8,128)(2,1)S(1)} %collective-permute-done.1.rest_2_), channel_id=1, source_target_pairs={{0,4},{4,0},{8,12},{12,8},{16,20},{20,16},{24,28},{28,24},{1,5},{5... | collective-permute-start | bytes 528392 | tf_op jit(solution)/shard_map/ppermute | solution.py:404
  25.1 7.0 %copy-start.5 = (bf16[368,128]{1,0:T(8,128)(2,1)}, bf16[368,128]{1,0:T(8,128)(2,1)S(1)}, u32[]{:S(2)}) copy-start(bf16[368,128]{1,0:T(8,128)(2,1)S(1)} %collective-permute-done.5.rest_6_) | copy-start | bytes 282628
  25.1 6.9 %collective-permute-start.6 = (bf16[368,128]{1,0:T(8,128)(2,1)S(1)}, bf16[368,128]{1,0:T(8,128)(2,1)S(1)}, u32[]{:S(2)}, u32[]{:S(2)}) collective-permute-start(bf16[368,128]{1,0:T(8,128)(2,1)S(1)} %collective-permute-done.5.rest_6_), channel_id=1, source_target_pairs={{0,4},{4,0},{8,12},{12,8},{16,20},{20,16},{24,28},{28,24},{1,5},{5... | collective-permute-start | bytes 282632 | tf_op jit(solution)/shard_map/ppermute | solution.py:404
  27.4 4.7 %copy-start.2 = (bf16[688,128]{1,0:T(8,128)(2,1)}, bf16[688,128]{1,0:T(8,128)(2,1)S(1)}, u32[]{:S(2)}) copy-start(bf16[688,128]{1,0:T(8,128)(2,1)S(1)} %collective-permute-done.rest_1_) | copy-start | bytes 528388
  32.0 0.6 %copy-start.6 = (bf16[368,128]{1,0:T(8,128)(2,1)}, bf16[368,128]{1,0:T(8,128)(2,1)S(1)}, u32[]{:S(2)}) copy-start(bf16[368,128]{1,0:T(8,128)(2,1)S(1)} %collective-permute-done.6.rest_7_) | copy-start | bytes 282628
  32.1 0.7 %copy-start.3 = (bf16[688,128]{1,0:T(8,128)(2,1)}, bf16[688,128]{1,0:T(8,128)(2,1)S(1)}, u32[]{:S(2)}) copy-start(bf16[688,128]{1,0:T(8,128)(2,1)S(1)} %collective-permute-done.4.rest_5_) | copy-start | bytes 528388
  32.7 0.7 %copy-start.4 = (bf16[688,128]{1,0:T(8,128)(2,1)}, bf16[688,128]{1,0:T(8,128)(2,1)S(1)}, u32[]{:S(2)}) copy-start(bf16[688,128]{1,0:T(8,128)(2,1)S(1)} %collective-permute-done.2.rest_3_) | copy-start | bytes 528388

commit v2 on v0

--- a/solution.py
+++ b/solution.py
@@ -1,6 +1,10 @@
+import functools
+
 import jax
 import jax.numpy as jnp
 from jax import lax
+from jax.experimental import pallas as pl
+from jax.experimental.pallas import tpu as pltpu
 from jax.sharding import PartitionSpec as P
 
 HEADS = 16
@@ -32,7 +36,7 @@
     return mixture.reshape(-1, head_count, value_rows.shape[1]) / totals[:, :, None]
 
 
-def body(queries, keys, values, gate_logits, sel_ids, pos_k, pos_v, mix_k, mix_v):
+def exchange_body(queries, keys, values, gate_logits, sel_ids, pos_k, pos_v, mix_k, mix_v):
     devices = lax.axis_size("ctx")
     myself = lax.axis_index("ctx")
     rounds = keys.shape[0]
@@ -200,6 +204,368 @@
     return combined.reshape(tokens, HEADS * DV).astype(jnp.bfloat16)
 
 
+PAIR = 2
+COMP_ROWS = 32
+PIECE_ROWS = DK + DV
+CACHED_ROWS = COMP_ROWS + PIECE_ROWS
+HALF = 64
+NEAR = 4
+NEAR_SLOTS = ((4, 4), (5, 3), (2, 2), (3, 1))
+BASE2_SCALE = DK ** (-0.5) * 1.4426950408889634
+NEVER = -jnp.inf
+KERNEL_PARAMS = pltpu.CompilerParams(vmem_limit_bytes=32 * 2**20)
+
+
+def pack_kernel(keys_t, values, pos_k, pos_v, mix_k, mix_v, whole, cached):
+    rounds, _, tokens = keys_t.shape
+    count = tokens // CMP_BLOCK
+    gains_k = jnp.concatenate([pos_k[...].astype(jnp.float32)] * count, axis=0).T
+    gains_v = jnp.concatenate([pos_v[...].astype(jnp.float32)] * count, axis=0)
+    pooled_k = jnp.zeros((DK, tokens), jnp.float32)
+    lane = lax.broadcasted_iota(jnp.int32, (tokens, tokens), 1)
+    segment = lax.broadcasted_iota(jnp.int32, (tokens, tokens), 0) // CMP_BLOCK
+    pooled_v = []
+    for piece in range(rounds):
+        base = COMP_ROWS + piece * PIECE_ROWS
+        for out in (whole, cached)[: 2 - piece]:
+            out[base : base + DK, :] = keys_t[piece]
+            out[base + DK : base + PIECE_ROWS, :] = values[piece]
+        product = keys_t[piece].astype(jnp.float32) * gains_k
+        upper = product.astype(jnp.bfloat16)
+        lower = (product - upper.astype(jnp.float32)).astype(jnp.bfloat16)
+        picks = (lane == segment + piece * count).astype(jnp.bfloat16)
+        pooled_k += jnp.dot(upper, picks, preferred_element_type=jnp.float32)
+        pooled_k += jnp.dot(lower, picks, preferred_element_type=jnp.float32)
+        product_v = values[piece].astype(jnp.float32) * gains_v
+        pooled_v.append(jnp.sum(product_v.reshape(count, CMP_BLOCK, DV), axis=1))
+    comp_k = lax.dot_general(
+        pooled_k.astype(jnp.bfloat16),
+        mix_k[...],
+        (((0,), (0,)), ((), ())),
+        preferred_element_type=jnp.float32,
+    )[: rounds * count]
+    comp_v = jnp.dot(
+        jnp.concatenate(pooled_v, axis=0).astype(jnp.bfloat16),
+        mix_v[...],
+        preferred_element_type=jnp.float32,
+    )
+    comp_k = jnp.concatenate([comp_k, jnp.zeros((rounds * count, HALF), jnp.float32)], axis=1)
+    rows = [comp_k[:, :DV], comp_k[:, DV:], comp_v]
+    rows.append(jnp.zeros((COMP_ROWS - 3 * rounds * count, DV), jnp.float32))
+    packed = jnp.concatenate(rows, axis=0).astype(jnp.bfloat16)
+    whole[:COMP_ROWS, :] = packed
+    cached[:COMP_ROWS, :] = packed
+
+
+def holder_of(slot, myself, devices):
+    source = lax.rem(myself // PAIR - slot // PAIR + devices // PAIR, devices // PAIR) * PAIR
+    side = lax.rem(myself, PAIR)
+    return source + (side if slot % PAIR == 0 else 1 - side)
+
+
+def add(scores, mask):
+    shape = (scores.shape[0] // mask.shape[0],) + mask.shape
+    return (scores.reshape(shape) + mask[None]).reshape(scores.shape)
+
+
+def prepare_kernel(devices, me_ref, gate_ref, sel_ref, gate_wide, bias, comp_bias):
+    groups = sel_ref.shape[0]
+    tokens = groups * QBLOCK
+    per_slot = 2 * tokens // CMP_BLOCK
+    myself = me_ref[0]
+    gates = jax.nn.sigmoid(gate_ref[...].astype(jnp.float32))
+    pad = jnp.zeros((2 * HALF - 3 * HEADS, tokens), jnp.float32)
+    gates = jnp.concatenate([gates, pad], axis=0).T
+    for column in range(3 * HEADS):
+        spread = jnp.broadcast_to(gates[:, column : column + 1], (tokens, DV))
+        gate_wide[:, column * DV : (column + 1) * DV] = spread
+    ids = sel_ref[...]
+    entry = lax.broadcasted_iota(jnp.int32, ids.shape, 1)
+    lane = lax.broadcasted_iota(jnp.int32, (groups, tokens), 1)
+    for slot in range(devices):
+        first = holder_of(slot, myself, devices) * (tokens // SEL_BLOCK)
+        row = jnp.full((groups, tokens), NEVER, jnp.float32)
+        for block in range(tokens // SEL_BLOCK):
+            found = jnp.where((ids == first + block) & (entry > 0), 1, 0)
+            named = jnp.max(found, axis=1, keepdims=True) > 0
+            row = jnp.where((lane // SEL_BLOCK == block) & named, 0.0, row)
+        spread = jnp.broadcast_to(row[:, None, :], (groups, QBLOCK, tokens))
+        bias[slot] = spread.reshape(tokens, tokens)
+    query = lax.broadcasted_iota(jnp.int32, (tokens, tokens), 0)
+    key_at = lax.broadcasted_iota(jnp.int32, (tokens, tokens), 1)
+    same = key_at // SEL_BLOCK == query // SEL_BLOCK
+    bias[devices] = jnp.where((key_at <= query) & same, 0.0, NEVER)
+    column = lax.broadcasted_iota(jnp.int32, comp_bias.shape, 1)
+    offset = lax.broadcasted_iota(jnp.int32, comp_bias.shape, 0)
+    within = lax.rem(column, per_slot) - per_slot // 2
+    ready = jnp.full(column.shape, -1, jnp.int32)
+    for slot in range(devices):
+        holder = holder_of(slot, myself, devices)
+        late = jnp.where(holder > myself, tokens, -1)
+        end = jnp.where(holder == myself, (within + 1) * CMP_BLOCK - 1, late)
+        ready = jnp.where((column // per_slot == slot) & (within >= 0), end, ready)
+    comp_bias[...] = jnp.where(ready <= offset, 0.0, NEVER)
+
+
+def attend_call(devices, slots, args, carried, messages):
+    me, queries, gate_wide, masks, comp_mask = args
+    first_pass = carried is None
+    tokens = queries.shape[0]
+    per_slot = 2 * tokens // CMP_BLOCK
+    near_width = (NEAR + 1) * tokens
+    far_width = (len(slots) + first_pass) * tokens
+    numbers = sorted(set(slots) | {0} if first_pass else messages)
+    step_heads, unit_heads, lag = (8, 2, 2) if first_pass else (8, 2, 1)
+    steps = HEADS // step_heads
+
+    def kernel(*refs):
+        refs = list(refs)
+        me_ref, q_ref, mask_ref = refs[:3]
+        del refs[:3]
+        gate_ref, comp_bias = (None, None) if first_pass else (refs.pop(0), refs.pop(0))
+        state = None if first_pass else [refs.pop(0) for _ in range(2)]
+        pieces = {slot: refs.pop(0) for slot in numbers}
+        outs = [refs.pop(0) for _ in range(2 if first_pass else 1)]
+        far_low, far_high, far_values = refs[:3]
+        if not first_pass:
+            near_low, near_high, near_values, comp_low, comp_high, comp_values = refs[3:]
+        tables = [(far_low, far_high, far_values)]
+        tables += [] if first_pass else [(near_low, near_high, near_values)]
+        myself = me_ref[0]
+        query = lax.broadcasted_iota(jnp.int32, (tokens, tokens), 0)
+        key_at = lax.broadcasted_iota(jnp.int32, (tokens, tokens), 1)
+
+        def stage(table, at, piece, start):
+            low, high, value = tables[table]
+            lanes = slice(at * tokens, (at + 1) * tokens)
+            part = piece[pl.ds(start, PIECE_ROWS), :]
+            low[:DK, lanes] = part[:DK]
+            high[HALF:, lanes] = part[:DK]
+            value[lanes, :DV] = part[DK:]
+
+        @pl.when(pl.program_id(0) == 0)
+        def _():
+            for low, high, value in tables:
+                nothing = jnp.zeros((HALF, low.shape[1]), jnp.bfloat16)
+                low[DK:, :] = nothing
+                high[:HALF, :] = nothing
+                value[:, DV:] = jnp.ones((value.shape[0], DV), jnp.bfloat16)
+            for at, slot in enumerate(slots):
+                stage(0, at, pieces[slot], COMP_ROWS)
+            if first_pass:
+                stage(0, len(slots), pieces[0], CACHED_ROWS)
+                return
+            side = lax.rem(myself, PAIR)
+            for place, choices in enumerate(NEAR_SLOTS):
+                in_span = (myself - (NEAR - place) >= 0).astype(jnp.int32)
+                start = pl.multiple_of(COMP_ROWS + in_span * PIECE_ROWS, 16)
+                if choices[0] == choices[1]:
+                    stage(1, place, pieces[choices[0]], start)
+                else:
+                    for value, slot in enumerate(choices):
+                        pl.when(side == value)(
+                            lambda place=place, slot=slot, start=start: stage(
+                                1, place, pieces[slot], start
+                            )
+                        )
+            stage(1, NEAR, pieces[0], CACHED_ROWS)
+            comp_values[:, DV:] = jnp.ones((devices * per_slot, DV), jnp.bfloat16)
+            for slot in numbers:
+                rows = slice(slot * per_slot, (slot + 1) * per_slot)
+                part = pieces[slot][:COMP_ROWS, :].astype(jnp.float32)
+                both = jnp.concatenate([part[:per_slot], part[per_slot : 2 * per_slot]], axis=1)
+                comp_low[rows, :] = both
+                comp_high[rows, :] = pltpu.roll(both, HALF, 1)
+                comp_values[rows, :DV] = part[2 * per_slot : 3 * per_slot].astype(jnp.bfloat16)
+
+        def gathered(ref, heads):
+            return jnp.concatenate([ref[:, h * DV : (h + 1) * DV] for h in heads], axis=0)
+
+        def score(odd, heads, kind):
+            rows = jnp.concatenate(
+                [q_ref[:, h * DK - odd * HALF : h * DK - odd * HALF + 2 * DV] for h in heads],
+                axis=0,
+            )
+            if kind == "far":
+                table = far_high if odd else far_low
+                scores = jnp.dot(rows, table[...], preferred_element_type=jnp.float32)
+                masks_of = list(slots) + [devices] * first_pass
+                bias = jnp.concatenate([mask_ref[slot] for slot in masks_of], axis=1)
+                return [add(scores, bias)]
+            if kind == "comp":
+                table = (comp_high if odd else comp_low)[...].astype(jnp.bfloat16)
+                scores = lax.dot_general(
+                    rows, table, (((1,), (1,)), ((), ())), preferred_element_type=jnp.float32
+                )
+                return [add(scores, comp_bias[...])]
+            table = near_high if odd else near_low
+            scores = jnp.dot(rows, table[...], preferred_element_type=jnp.float32)
+            return [
+                add(scores[:, :tokens], jnp.where(key_at > query, 0.0, NEVER)),
+                scores[:, tokens : NEAR * tokens],
+                add(scores[:, NEAR * tokens :], jnp.where(key_at <= query, 0.0, NEVER)),
+            ]
+
+        def weigh(heads, kind, scores):
+            highest = scores[0].max(axis=1, keepdims=True)
+            for part in scores[1:]:
+                highest = jnp.maximum(highest, part.max(axis=1, keepdims=True))
+            if kind == "far":
+                highest = jnp.broadcast_to(highest, (highest.shape[0], DV))
+                if not first_pass:
+                    highest = jnp.maximum(highest, gathered(state[1], heads))
+                wide = jnp.concatenate([highest] * (scores[0].shape[1] // DV), axis=1)
+            else:
+                wide = highest
+            weights = [jnp.exp2((part - wide) * BASE2_SCALE).astype(jnp.bfloat16) for part in scores]
+            return highest, weights
+
+        def mix(heads, kind, highest, weights):
+            taken = jnp.concatenate(weights, axis=1) if len(weights) > 1 else weights[0]
+            value = far_values if kind == "far" else near_values if kind == "near" else comp_values
+            both = jnp.dot(taken, value[...], preferred_element_type=jnp.float32)
+            mixed, total = both[:, :DV], both[:, DV:]
+            if kind == "far" and not first_pass:
+                fade = jnp.exp2((gathered(state[1], heads) - highest) * BASE2_SCALE)
+                mixed, total = mixed + gathered(state[0], heads) * fade, total + fade
+            if kind == "far" and first_pass:
+                return mixed / total, highest + jnp.log(total) * DK**0.5
+            return mixed / total
+
+        kinds = ("far",) if first_pass else ("comp", "far", "near")
+        units = []
+        for odd in range(2):
+            for first in range(odd, step_heads, unit_heads * 2):
+                heads = list(range(first, first + 2 * unit_heads, 2))
+                units += [(odd, heads, kind) for kind in kinds[::-1]]
+        found, scored, weighed = {}, {}, {}
+        for turn in range(len(units) + 2 * lag):
+            if turn < len(units):
+                scored[turn] = score(*units[turn])
+            at = turn - lag
+            if 0 <= at < len(units):
+                weighed[at] = weigh(*units[at][1:], scored.pop(at))
+            at = turn - 2 * lag
+            if 0 <= at < len(units):
+                _, heads, kind = units[at]
+                found[kind] = mix(heads, kind, *weighed.pop(at))
+                if len(found) < len(kinds):
+                    continue
+                for which, head in enumerate(heads):
+                    lines = slice(which * tokens, (which + 1) * tokens)
+                    cols = slice(head * DV, (head + 1) * DV)
+                    if first_pass:
+                        for out, part in zip(outs, found["far"]):
+                            out[:, cols] = part[lines]
+                        continue
+                    total = 0.0
+                    for b, kind in enumerate(kinds):
+                        column = b * HEADS + head + step_heads * pl.program_id(0)
+                        lanes = pl.ds(pl.multiple_of(column * DV, DV), DV)
+                        total += gate_ref[:, lanes] * found[kind][lines]
+                    outs[0][:, cols] = total.astype(jnp.bfloat16)
+                found = {}
+
+    in_vmem = pl.BlockSpec(memory_space=pltpu.VMEM)
+    by_head = pl.BlockSpec((tokens, step_heads * DV), lambda i: (0, i))
+    in_specs = [
+        pl.BlockSpec(memory_space=pltpu.SMEM),
+        pl.BlockSpec((tokens, step_heads * DK), lambda i: (0, i)),
+        in_vmem,
+    ]
+    operands = [me, queries, masks]
+    if not first_pass:
+        in_specs += [in_vmem] * 2
+        operands += [gate_wide, comp_mask]
+    if not first_pass:
+        in_specs += [by_head] * 2
+        operands += carried
+    for slot in numbers:
+        in_specs.append(in_vmem)
+        operands.append(pltpu.with_memory_space_constraint(messages[slot], pltpu.VMEM))
+    scratch = [
+        pltpu.VMEM((2 * DV, far_width), jnp.bfloat16),
+        pltpu.VMEM((2 * DV, far_width), jnp.bfloat16),
+        pltpu.VMEM((far_width, 2 * DV), jnp.bfloat16),
+    ]
+    if not first_pass:
+        scratch += [
+            pltpu.VMEM((2 * DV, near_width), jnp.bfloat16),
+            pltpu.VMEM((2 * DV, near_width), jnp.bfloat16),
+            pltpu.VMEM((near_width, 2 * DV), jnp.bfloat16),
+            pltpu.VMEM((devices * per_slot, 2 * DV), jnp.float32),
+            pltpu.VMEM((devices * per_slot, 2 * DV), jnp.float32),
+            pltpu.VMEM((devices * per_slot, 2 * DV), jnp.bfloat16),
+        ]
+    partial = [jax.ShapeDtypeStruct((tokens, HEADS * DV), jnp.float32)] * 2
+    columns = far_width if first_pass else far_width + near_width
+    return pl.pallas_call(
+        kernel,
+        grid=(steps,),
+        in_specs=in_specs,
+        out_specs=[by_head] * 2 if first_pass else by_head,
+        out_shape=partial if first_pass else jax.ShapeDtypeStruct((tokens, HEADS * DV), jnp.bfloat16),
+        scratch_shapes=scratch,
+        cost_estimate=pl.CostEstimate(
+            flops=2 * tokens * HEADS * columns * (DK + DV),
+            transcendentals=tokens * HEADS * columns,
+            bytes_accessed=2 * queries.size,
+        ),
+        compiler_params=KERNEL_PARAMS,
+    )(*operands)
+
+
+EARLY = (0, 1, 2, 3, 4, 6)
+
+
+def dense_body(queries, keys, values, gate_logits, sel_ids, pos_k, pos_v, mix_k, mix_v):
+    devices = lax.axis_size("ctx")
+    tokens = keys.shape[1]
+    rows = CACHED_ROWS + PIECE_ROWS
+    message, cached = pl.pallas_call(
+        pack_kernel,
+        out_shape=[
+            jax.ShapeDtypeStruct((rows, tokens), jnp.bfloat16),
+            jax.ShapeDtypeStruct((CACHED_ROWS, tokens), jnp.bfloat16),
+        ],
+        name="pack",
+    )(jnp.swapaxes(keys, 1, 2), values, pos_k, pos_v, mix_k, mix_v)
+
+    in_vmem = pl.BlockSpec(memory_space=pltpu.VMEM)
+    messages = {0: message}
+    for slot in range(2, devices, PAIR):
+        sent = message if slot <= 4 else cached
+        messages[slot] = shifted(sent, "ctx", slot)
+    for slot in range(0, devices, PAIR):
+        pairs = [(i, i ^ 1) for i in range(devices)]
+        messages[slot + 1] = lax.ppermute(messages[slot], "ctx", pairs)
+    me = lax.axis_index("ctx").astype(jnp.int32).reshape(1)
+    prepared = pl.pallas_call(
+        functools.partial(prepare_kernel, devices),
+        in_specs=[pl.BlockSpec(memory_space=pltpu.SMEM)] + [in_vmem] * 2,
+        out_specs=[in_vmem] * 3,
+        out_shape=[
+            pltpu.VMEM((tokens, 3 * HEADS * DV), jnp.float32),
+            pltpu.VMEM((devices + 1, tokens, tokens), jnp.float32),
+            pltpu.VMEM((tokens, devices * 2 * tokens // CMP_BLOCK), jnp.float32),
+        ],
+        name="prepare", compiler_params=KERNEL_PARAMS,
+    )(me, gate_logits.T, sel_ids)
+    args = (me, queries, *prepared)
+    late = tuple(slot for slot in messages if slot not in EARLY)
+    state = attend_call(devices, EARLY, args, None, messages)
+    return attend_call(devices, sorted(late), args, state, messages)
+
+
+def body(queries, keys, *others):
+    devices = lax.axis_size("ctx")
+    rounds, tokens = keys.shape[:2]
+    blocks = (rounds - 1) * tokens // SEL_BLOCK * devices
+    dense = rounds == 2 and blocks <= SPREAD and devices % PAIR == 0 and devices >= 6
+    chosen = dense_body if dense else exchange_body
+    return chosen(queries, keys, *others)
+
+
 def solution(mesh):
     in_specs = (
         P("ctx", "grp"),

time: 187 us -> 35.5 us (0.19)
  blocking collectives: 57.5 us -> 0 us
  local copies, waits for them, and re-layouts: 57.5 us -> 3.45 us
  other arithmetic: 25.6 us -> 0 us
  matrix products: 20.8 us -> 0 us
  Pallas kernels: 0 us -> 12.4 us
  starting transfers between devices: 23.6 us -> 11.9 us
  waiting for transfers between devices: 0.02 us -> 7.39 us
    all_gather x2 -> x0, blocking collectives: 57.5 us -> none  [the longest x1 30.6 us: body(): lax.all_gather(comp_keys, 'ctx', axis=0, tiled=True)]
    dot_general x8 -> x0, matrix products: 20.8 us -> none  [the longest x1 7.63 us: body(): jnp.einsum('aqk,akd->aqd', weights.astype(jnp.bfloat16).reshape(groups, Q...]
    all_to_all x3 -> x0, starting transfers between devices: 17.2 us -> none  [the longest x1 7.29 us: body(): lax.all_to_all(requests.reshape(devices, per_owner), 'ctx', split_axis=0,...]
    reshape x7 -> x0, local copies, waits for them, and re-layouts: 12.6 us -> none  [the longest x1 3 us: body(): grouped_q = queries.reshape(groups, QBLOCK * HEADS, DK)]
    pallas_call x0 -> x4, Pallas kernels: none -> 12.4 us  [the longest x2 9.08 us: attend_call(): pl.pallas_call(kernel, grid=(steps,), in_specs=in_specs, out_specs=[by_he...]
    gather x7 -> x0, local copies, waits for them, and re-layouts: 11.8 us -> none  [the longest x1 3.03 us: body(): near_keys = got_keys.reshape(devices * per_owner, SEL_BLOCK, DK)[fetch_at]]
    broadcast_in_dim x9 -> x0, local copies, waits for them, and re-layouts: 8.07 us -> none  [the longest x2 4.58 us: body(): jnp.where(allowed[:, :, None, :], scores.reshape(groups, QBLOCK, HEADS, k...]
    reduce_sum x4 -> x0, other arithmetic: 7.97 us -> none  [the longest x1 4.81 us: attention(): totals = jnp.sum(weights, axis=2)]
  transfers between devices with their start and end apart: 7 -> 7, of which waited for: 0 -> 2; matrix products, arithmetic and copies ran while one was open for 38% -> 0% of each run, Pallas kernels for 0% -> 14%
where the time goes in v2:
time: 35.5 us; the launch traced here: 35.2 us
  Pallas kernels  12.4 us (35%)
  starting transfers between devices  11.9 us (34%)
  waiting for transfers between devices  7.39 us (21%)
  local copies, waits for them, and re-layouts  3.45 us (10%)
    pallas_call x2, Pallas kernels, attend_call(): pl.pallas_call(kernel, grid=(steps,), in_specs=in_specs, out_specs=[by_he...  9.08 us
    ppermute x3, waiting for transfers between devices, shifted(): return lax.ppermute(value, axis, pairs)  7.38 us
    ppermute x3, starting transfers between devices, shifted(): return lax.ppermute(value, axis, pairs)  6.59 us
    ppermute x4, starting transfers between devices, dense_body(): messages[slot + 1] = lax.ppermute(messages[slot], 'ctx', pairs)  5.29 us
    unnamed x10, local copies, waits for them, and re-layouts  3.45 us
    pallas_call x1, Pallas kernels, dense_body(): pl.pallas_call(pack_kernel, out_shape=[jax.ShapeDtypeStruct((rows, tokens...  2.19 us
    pallas_call x1, Pallas kernels, dense_body(): pl.pallas_call(functools.partial(prepare_kernel, devices), in_specs=[pl.B...  1.18 us
  transfers between devices with their start and end apart: 7, of which 2 were waited for; matrix products, arithmetic and copies ran while one was open for 0% of the time, Pallas kernels for 14%

profile of v2, /device:TPU:0, one launch (start us, length us, event | category | flops | bytes accessed | tf_op | source)
XLA Modules:
  0.0 35.2 jit_solution(14384699662066384193)
XLA Ops:
  0.0 2.2 %pack.1 = (bf16[672,128]{1,0:T(8,128)(2,1)}, bf16[352,128]{1,0:T(8,128)(2,1)}) custom-call(bf16[2,192,128]{2,1,0:T(8,128)(2,1)} %bitcast.4, bf16[2,128,128]{2,1,0:T(8,128)(2,1)} %values.1, bf16[32,192]{1,0:T(8,128)(2,1)} %pos_k.1, bf16[32,128]{1,0:T(8,128)(2,1)} %pos_v.1, bf16[192,192]{1,0:T(8,128)(2,1)} %mix_k.1, bf16[128,128]{1,0:T(8,128)(2,1)} %mix_v.1), custom_call_target="tpu_custom_call" | custom-call | tf_op jit(solution)/shard_map/pack/pallas_call | solution.py:525
  2.2 3.1 %collective-permute-start.1 = (bf16[672,128]{1,0:T(8,128)(2,1)}, bf16[672,128]{1,0:T(8,128)(2,1)S(1)}, u32[]{:S(2)}, u32[]{:S(2)}) collective-permute-start(bf16[672,128]{1,0:T(8,128)(2,1)} %get-tuple-element.15.refs_3_.refs_7_), channel_id=1, source_target_pairs={{0,8},{4,12},{8,16},{12,20},{16,24},{20,28},{24,0},{28,4},{1,9},{5... | collective-permute-start | bytes 516104 | tf_op jit(solution)/shard_map/ppermute | solution.py:22
  5.2 2.6 %collective-permute-start.3 = (bf16[672,128]{1,0:T(8,128)(2,1)}, bf16[672,128]{1,0:T(8,128)(2,1)S(1)}, u32[]{:S(2)}, u32[]{:S(2)}) collective-permute-start(bf16[672,128]{1,0:T(8,128)(2,1)} %get-tuple-element.15.refs_3_.refs_7_), channel_id=1, source_target_pairs={{0,16},{4,20},{8,24},{12,28},{16,0},{20,4},{24,8},{28,12},{1,17},{... | collective-permute-start | bytes 516104 | tf_op jit(solution)/shard_map/ppermute | solution.py:22
  7.8 1.5 %collective-permute-start = (bf16[672,128]{1,0:T(8,128)(2,1)}, bf16[672,128]{1,0:T(8,128)(2,1)S(1)}, u32[]{:S(2)}, u32[]{:S(2)}) collective-permute-start(bf16[672,128]{1,0:T(8,128)(2,1)} %get-tuple-element.15.refs_3_.refs_7_), channel_id=1, source_target_pairs={{0,4},{4,0},{8,12},{12,8},{16,20},{20,16},{24,28},{28,24},{1,5},{5... | collective-permute-start | bytes 516104 | tf_op jit(solution)/shard_map/ppermute | solution.py:541
  9.3 3.5 %collective-permute-done.1.refs_5_.refs_9_ = bf16[672,128]{1,0:T(8,128)(2,1)S(1)} collective-permute-done((bf16[672,128]{1,0:T(8,128)(2,1)}, bf16[672,128]{1,0:T(8,128)(2,1)S(1)}, u32[]{:S(2)}, u32[]{:S(2)}) %collective-permute-start.1) | collective-permute-done | bytes 172064 | tf_op jit(solution)/shard_map/ppermute | solution.py:22
  12.8 1.7 %collective-permute-start.2 = (bf16[672,128]{1,0:T(8,128)(2,1)S(1)}, bf16[672,128]{1,0:T(8,128)(2,1)S(1)}, u32[]{:S(2)}, u32[]{:S(2)}) collective-permute-start(bf16[672,128]{1,0:T(8,128)(2,1)S(1)} %collective-permute-done.1.refs_5_.refs_9_), channel_id=1, source_target_pairs={{0,4},{4,0},{8,12},{12,8},{16,20},{20,16},{24,28},{28,24},{1,5},{5... | collective-permute-start | bytes 516104 | tf_op jit(solution)/shard_map/ppermute | solution.py:541
  14.5 0.9 %collective-permute-start.4 = (bf16[352,128]{1,0:T(8,128)(2,1)}, bf16[352,128]{1,0:T(8,128)(2,1)S(1)}, u32[]{:S(2)}, u32[]{:S(2)}) collective-permute-start(bf16[352,128]{1,0:T(8,128)(2,1)} %get-tuple-element.16), channel_id=1, source_target_pairs={{0,24},{4,28},{8,0},{12,4},{16,8},{20,12},{24,16},{28,20},{1,25},{... | collective-permute-start | bytes 270344 | tf_op jit(solution)/shard_map/ppermute | solution.py:22
  15.5 3.9 %collective-permute-done.3.refs_7_.refs_11_ = bf16[672,128]{1,0:T(8,128)(2,1)S(1)} collective-permute-done((bf16[672,128]{1,0:T(8,128)(2,1)}, bf16[672,128]{1,0:T(8,128)(2,1)S(1)}, u32[]{:S(2)}, u32[]{:S(2)}) %collective-permute-start.3) | collective-permute-done | bytes 172064 | tf_op jit(solution)/shard_map/ppermute | solution.py:22
  19.4 1.5 %collective-permute-start.5 = (bf16[672,128]{1,0:T(8,128)(2,1)S(1)}, bf16[672,128]{1,0:T(8,128)(2,1)S(1)}, u32[]{:S(2)}, u32[]{:S(2)}) collective-permute-start(bf16[672,128]{1,0:T(8,128)(2,1)S(1)} %collective-permute-done.3.refs_7_.refs_11_), channel_id=1, source_target_pairs={{0,4},{4,0},{8,12},{12,8},{16,20},{20,16},{24,28},{28,24},{1,5},{5... | collective-permute-start | bytes 516104 | tf_op jit(solution)/shard_map/ppermute | solution.py:541
  20.8 0.0 copy-start.3
  20.8 0.7 %copy-done.3 = bf16[128,48]{0,1:T(8,128)(2,1)S(1)} copy-done((bf16[128,48]{0,1:T(8,128)(2,1)S(1)}, bf16[128,48]{0,1:T(8,128)(2,1)}, u32[]{:S(2)}) %copy-start.3) | copy-done | bytes 12312
  21.5 0.0 copy-start.4
  21.5 0.7 %copy-done.4 = s32[8,16]{1,0:T(8,128)S(1)} copy-done((s32[8,16]{1,0:T(8,128)S(1)}, s32[8,16]{1,0:T(8,128)}, u32[]{:S(2)}) %copy-start.4) | copy-done | bytes 536
  22.2 1.2 %prepare.1 = (f32[128,6144]{1,0:T(8,128)S(1)}, f32[9,128,128]{2,1,0:T(8,128)S(1)}, f32[128,64]{1,0:T(8,128)S(1)}) custom-call(s32[1]{0:T(128)} %bitcast.me_ref.refs_0_, bf16[48,128]{1,0:T(8,128)(2,1)S(1)} %bitcast.3, s32[8,16]{1,0:T(8,128)S(1)} %copy-done.4), custom_call_target="tpu_custom_call" | custom-call | tf_op jit(solution)/shard_map/prepare/pallas_call | solution.py:543
  23.4 0.0 collective-permute-done.4.refs_8_.refs_13_
  23.4 0.6 %collective-permute-start.6 = (bf16[352,128]{1,0:T(8,128)(2,1)S(1)}, bf16[352,128]{1,0:T(8,128)(2,1)S(1)}, u32[]{:S(2)}, u32[]{:S(2)}) collective-permute-start(bf16[352,128]{1,0:T(8,128)(2,1)S(1)} %collective-permute-done.4.refs_8_.refs_13_), channel_id=1, source_target_pairs={{0,4},{4,0},{8,12},{12,8},{16,20},{20,16},{24,28},{28,24},{1,5},{5... | collective-permute-start | bytes 270344 | tf_op jit(solution)/shard_map/ppermute | solution.py:541
  24.0 0.0 collective-permute-done.refs_4_.refs_8_
  24.0 0.0 collective-permute-done.2.refs_6_.refs_10_
  24.1 0.0 copy-start
  24.1 1.1 %copy-done = bf16[128,3072]{1,0:T(8,128)(2,1)S(1)} copy-done((bf16[128,3072]{1,0:T(8,128)(2,1)S(1)}, bf16[128,3072]{1,0:T(8,128)(2,1)}, u32[]{:S(2)}) %copy-start) | copy-done | bytes 786456
  25.2 0.0 copy-start.1
  25.2 0.9 %copy-done.1 = bf16[672,128]{1,0:T(8,128)(2,1)S(1)} copy-done((bf16[672,128]{1,0:T(8,128)(2,1)S(1)}, bf16[672,128]{1,0:T(8,128)(2,1)}, u32[]{:S(2)}) %copy-start.1) | copy-done | bytes 172056
  26.1 0.0 copy-start.2
  26.1 3.8 %shard_map.91 = (f32[128,2048]{1,0:T(8,128)S(1)}, f32[128,2048]{1,0:T(8,128)S(1)}) custom-call(s32[1]{0:T(128)} %bitcast.me_ref.refs_0_, bf16[128,3072]{1,0:T(8,128)(2,1)S(1)} %copy-done, f32[9,128,128]{2,1,0:T(8,128)S(1)} %get-tuple-element.12.refs_2_, bf16[672,128]{1,0:T(8,128)(2,1)S(1)} %copy-done.1, ...), custom_call_target="tpu_custom_call" | custom-call | flops 1174405120 | bytes 786432 | tf_op jit(solution)/shard_map/pallas_call | solution.py:502
  30.0 0.0 collective-permute-done.6.refs_14_
  30.0 0.0 collective-permute-done.5.refs_12_
  30.0 0.0 copy-done.2
  30.0 5.2 %shard_map.92 = bf16[128,2048]{1,0:T(8,128)(2,1)} custom-call(s32[1]{0:T(128)} %bitcast.me_ref.refs_0_, bf16[128,3072]{1,0:T(8,128)(2,1)S(1)} %copy-done, f32[9,128,128]{2,1,0:T(8,128)S(1)} %get-tuple-element.12.refs_2_, f32[128,6144]{1,0:T(8,128)S(1)} %get-tuple-element.13.refs_3_, f32[128,64]{1,0:T(8,128)S(1)} %get-tuple-element.14.refs_4_, ...), custom_call_target="tpu_custom_call" | custom-call | flops 1174405120 | bytes 786432 | tf_op jit(solution)/shard_map/pallas_call | solution.py:502
Async XLA Ops:
  2.2 10.6 %collective-permute-start.1 = (bf16[672,128]{1,0:T(8,128)(2,1)}, bf16[672,128]{1,0:T(8,128)(2,1)S(1)}, u32[]{:S(2)}, u32[]{:S(2)}) collective-permute-start(bf16[672,128]{1,0:T(8,128)(2,1)} %get-tuple-element.15.refs_3_.refs_7_), channel_id=1, source_target_pairs={{0,8},{4,12},{8,16},{12,20},{16,24},{20,28},{24,0},{28,4},{1,9},{5... | collective-permute-start | bytes 516104 | tf_op jit(solution)/shard_map/ppermute | solution.py:22
  5.2 14.1 %collective-permute-start.3 = (bf16[672,128]{1,0:T(8,128)(2,1)}, bf16[672,128]{1,0:T(8,128)(2,1)S(1)}, u32[]{:S(2)}, u32[]{:S(2)}) collective-permute-start(bf16[672,128]{1,0:T(8,128)(2,1)} %get-tuple-element.15.refs_3_.refs_7_), channel_id=1, source_target_pairs={{0,16},{4,20},{8,24},{12,28},{16,0},{20,4},{24,8},{28,12},{1,17},{... | collective-permute-start | bytes 516104 | tf_op jit(solution)/shard_map/ppermute | solution.py:22
  7.8 16.2 %collective-permute-start = (bf16[672,128]{1,0:T(8,128)(2,1)}, bf16[672,128]{1,0:T(8,128)(2,1)S(1)}, u32[]{:S(2)}, u32[]{:S(2)}) collective-permute-start(bf16[672,128]{1,0:T(8,128)(2,1)} %get-tuple-element.15.refs_3_.refs_7_), channel_id=1, source_target_pairs={{0,4},{4,0},{8,12},{12,8},{16,20},{20,16},{24,28},{28,24},{1,5},{5... | collective-permute-start | bytes 516104 | tf_op jit(solution)/shard_map/ppermute | solution.py:541
  12.8 11.2 %collective-permute-start.2 = (bf16[672,128]{1,0:T(8,128)(2,1)S(1)}, bf16[672,128]{1,0:T(8,128)(2,1)S(1)}, u32[]{:S(2)}, u32[]{:S(2)}) collective-permute-start(bf16[672,128]{1,0:T(8,128)(2,1)S(1)} %collective-permute-done.1.refs_5_.refs_9_), channel_id=1, source_target_pairs={{0,4},{4,0},{8,12},{12,8},{16,20},{20,16},{24,28},{28,24},{1,5},{5... | collective-permute-start | bytes 516104 | tf_op jit(solution)/shard_map/ppermute | solution.py:541
  14.5 8.9 %collective-permute-start.4 = (bf16[352,128]{1,0:T(8,128)(2,1)}, bf16[352,128]{1,0:T(8,128)(2,1)S(1)}, u32[]{:S(2)}, u32[]{:S(2)}) collective-permute-start(bf16[352,128]{1,0:T(8,128)(2,1)} %get-tuple-element.16), channel_id=1, source_target_pairs={{0,24},{4,28},{8,0},{12,4},{16,8},{20,12},{24,16},{28,20},{1,25},{... | collective-permute-start | bytes 270344 | tf_op jit(solution)/shard_map/ppermute | solution.py:22
  19.4 10.6 %collective-permute-start.5 = (bf16[672,128]{1,0:T(8,128)(2,1)S(1)}, bf16[672,128]{1,0:T(8,128)(2,1)S(1)}, u32[]{:S(2)}, u32[]{:S(2)}) collective-permute-start(bf16[672,128]{1,0:T(8,128)(2,1)S(1)} %collective-permute-done.3.refs_7_.refs_11_), channel_id=1, source_target_pairs={{0,4},{4,0},{8,12},{12,8},{16,20},{20,16},{24,28},{28,24},{1,5},{5... | collective-permute-start | bytes 516104 | tf_op jit(solution)/shard_map/ppermute | solution.py:541
  20.8 0.7 %copy-start.3 = (bf16[128,48]{0,1:T(8,128)(2,1)S(1)}, bf16[128,48]{0,1:T(8,128)(2,1)}, u32[]{:S(2)}) copy-start(bf16[128,48]{0,1:T(8,128)(2,1)} %param.12) | copy-start | bytes 36868
  21.5 0.7 %copy-start.4 = (s32[8,16]{1,0:T(8,128)S(1)}, s32[8,16]{1,0:T(8,128)}, u32[]{:S(2)}) copy-start(s32[8,16]{1,0:T(8,128)} %sel_ref.1) | copy-start | bytes 1540
  23.4 6.6 %collective-permute-start.6 = (bf16[352,128]{1,0:T(8,128)(2,1)S(1)}, bf16[352,128]{1,0:T(8,128)(2,1)S(1)}, u32[]{:S(2)}, u32[]{:S(2)}) collective-permute-start(bf16[352,128]{1,0:T(8,128)(2,1)S(1)} %collective-permute-done.4.refs_8_.refs_13_), channel_id=1, source_target_pairs={{0,4},{4,0},{8,12},{12,8},{16,20},{20,16},{24,28},{28,24},{1,5},{5... | collective-permute-start | bytes 270344 | tf_op jit(solution)/shard_map/ppermute | solution.py:541
  24.1 1.1 %copy-start = (bf16[128,3072]{1,0:T(8,128)(2,1)S(1)}, bf16[128,3072]{1,0:T(8,128)(2,1)}, u32[]{:S(2)}) copy-start(bf16[128,3072]{1,0:T(8,128)(2,1)} %refs_1_.3) | copy-start | bytes 2359300
  25.2 0.9 %copy-start.1 = (bf16[672,128]{1,0:T(8,128)(2,1)S(1)}, bf16[672,128]{1,0:T(8,128)(2,1)}, u32[]{:S(2)}) copy-start(bf16[672,128]{1,0:T(8,128)(2,1)} %get-tuple-element.15.refs_3_.refs_7_) | copy-start | bytes 516100
  26.1 3.9 %copy-start.2 = (bf16[672,128]{1,0:T(8,128)(2,1)S(1)}, bf16[672,128]{1,0:T(8,128)(2,1)}, u32[]{:S(2)}) copy-start(bf16[672,128]{1,0:T(8,128)(2,1)} %get-tuple-element.15.refs_3_.refs_7_) | copy-start | bytes 516100
